TPU v7x, 256 devices: a whole 4x4x8 slice. The times are simulated.
256 devices in a mesh: gx: 8 (over x, core), gy: 4 (over y), gz: 8 (over z).
Axes of the slice: x: 4, y: 4, z: 8, core: 2. Of those that a mesh axis runs over, the one named last changes fastest.
Arguments:
- right_side: float32 [128, 512, 512], P('gx', 'gz', 'gy'), may hold values from -8 to 8, as said below
- absorption: float32 [128, 512, 512], P('gx', 'gz', 'gy'), may hold values from 1e-05 to 1, as said below
Outputs:
- fine_iterate: float32 [128, 512, 512], P('gx', 'gz', 'gy')
- middle_iterate: float32 [64, 256, 256], P('gx', 'gz', 'gy')
- corrected_iterate: float32 [32, 128, 128], P('gx', 'gz', 'gy')
Inputs may be any that keep to these rules, and one draw needn't show every extreme that they name: `right_side`: independent cell values, possibly with a smooth part added. `absorption`: positive at every cell.
All inputs are finite; a program needn't handle non-finite values.
Results may differ from a plain program's by a relative error of at most 0.0001.
Values sent between devices are 32-bit elements; how exact they have to be, the bound alone decides.
No kernel may reach another device: no remote copies, remote signals or barrier semaphores. Data moves between devices by JAX's collectives and lax.ppermute only.
A program may use at most 128 MiB of HBM per device.

v0:
```python
import jax
import jax.numpy as jnp
from jax import lax
from jax.sharding import PartitionSpec as P

DEGREE = 4
LEVELS = 3
BOTTOM_ITERS = 20


smooth_low = 1.5
smooth_top = 12.0
absorb_top = 1.0
bottom_low = 0.008


def extended_2(cells, sides, width):
    for axis, dim in sides:
        count = lax.axis_size(axis)
        ends = count - 1
        head = lax.slice_in_dim(cells, 0, width, axis=dim)
        tail = lax.slice_in_dim(cells, cells.shape[dim] - width, cells.shape[dim], axis=dim)
        cells = jnp.concatenate(
            [
                lax.ppermute(tail, axis, [(i, (i + 1) % count) for i in range(ends)]),
                cells,
                lax.ppermute(head, axis, [((i + 1) % count, i) for i in range(ends)]),
            ],
            axis=dim,
        )
    return cells


def from_partner(value, axis, bit):
    mask = 2**bit
    pairs = [(source, source ^ mask) for source in range(lax.axis_size(axis))]
    return lax.ppermute(value, axis, pairs)


def cheb_tables(count, lower, upper):
    theta = (upper + lower) / 2.0
    delta = (upper - lower) / 2.0
    sigma = theta / delta
    rho_value = 1.0 / sigma
    firsts = []
    seconds = []
    for turn_index in range(count - 1):
        rho_next = 1.0 / (2.0 * sigma - rho_value)
        firsts.append(rho_next * rho_value)
        seconds.append(2.0 * rho_next / delta)
        rho_value = rho_next
    return (1.0 / theta, firsts, seconds)


def chebyshev(source, coefficient, count, lower, upper, operate):
    start_scale, firsts, seconds = cheb_tables(count, lower, upper)
    first_table = jnp.asarray(firsts, jnp.float32)
    second_table = jnp.asarray(seconds, jnp.float32)
    direction = source * start_scale

    def turn(turn_index, carry):
        iterate, direction, residual = carry
        residual = residual - operate(direction, coefficient)
        direction = first_table[turn_index] * direction + second_table[turn_index] * residual
        return (iterate + direction, direction, residual)

    iterate, direction, residual = lax.fori_loop(0, count - 1, turn, (direction, direction, source))
    return iterate


def neighbours(padded):
    return (
        padded[2:, 1:-1, 1:-1]
        + padded[:-2, 1:-1, 1:-1]
        + padded[1:-1, 2:, 1:-1]
        + padded[1:-1, :-2, 1:-1]
        + padded[1:-1, 1:-1, 2:]
        + padded[1:-1, 1:-1, :-2]
    )


def thin_operator(field, coefficient):
    padded = extended_2(field, (("gx", 0), ("gy", 2), ("gz", 1)), 1)
    return (6.0 + coefficient) * field - neighbours(padded)


def restrict_four(field):
    first, second, third = field.shape
    blocks = field.reshape(first // 2, 2, second // 2, 2, third // 2, 2)
    return blocks.sum(axis=(1, 3, 5)) * 0.5


def prolong_axis(extended, axis):
    count = extended.shape[axis] - 2
    center = lax.slice_in_dim(extended, 1, count + 1, axis=axis)
    lower = lax.slice_in_dim(extended, 0, count, axis=axis)
    upper = lax.slice_in_dim(extended, 2, count + 2, axis=axis)
    even = 0.75 * center + 0.25 * lower
    odd = 0.75 * center + 0.25 * upper
    stacked = jnp.stack((even, odd), axis=axis + 1)
    shape = list(extended.shape)
    shape[axis] = 2 * count
    return stacked.reshape(shape)


def prolong(extended):
    for axis in range(3):
        extended = prolong_axis(extended, axis)
    return extended


def join_pair(mine, partner, index, bit, dim):
    upper_half = index // 2**bit % 2 == 1
    return jnp.where(
        upper_half, jnp.concatenate((partner, mine), dim), jnp.concatenate((mine, partner), dim)
    )


def extend_bottom(field):
    padded = extended_2(field, (("gy", 2), ("gz", 1)), 1)
    return jnp.pad(padded, ((1, 1), (0, 0), (0, 0)))


def bottom_operator(field, coefficient):
    return (6.0 + coefficient) * field - neighbours(extend_bottom(field))


def on_device(right_side, absorption):
    source = right_side
    coefficient = absorption
    iterates = []
    for section in range(LEVELS):
        upper_bound = smooth_top + 4.0**section * absorb_top
        iterate = chebyshev(source, coefficient, DEGREE + 1, smooth_low, upper_bound, thin_operator)
        padded = extended_2(iterate, (("gx", 0), ("gy", 2), ("gz", 1)), 1)
        residual = source - ((6.0 + coefficient) * iterate - neighbours(padded))
        iterates.append(iterate)
        source = restrict_four(residual)
        coefficient = restrict_four(coefficient)
    folded = jnp.stack((source, coefficient))
    for bit in range(lax.axis_size("gx").bit_length() - 1):
        partner = from_partner(folded, "gx", bit)
        folded = join_pair(folded, partner, lax.axis_index("gx"), bit, 1)
    bottom_top = smooth_top + 4.0**LEVELS * absorb_top
    correction = chebyshev(
        folded[0], folded[1], BOTTOM_ITERS, bottom_low, bottom_top, bottom_operator
    )
    extended = extend_bottom(correction)
    block_first = source.shape[0]
    window = lax.dynamic_slice_in_dim(
        extended, lax.axis_index("gx") * block_first, block_first + 2, 0
    )
    corrected = iterates[2] + prolong(window)
    return (iterates[0], iterates[1], corrected)


def solution(mesh):
    placed = (P("gx", "gz", "gy"), P("gx", "gz", "gy"))
    return jax.shard_map(
        on_device,
        mesh=mesh,
        in_specs=placed,
        out_specs=(P("gx", "gz", "gy"), P("gx", "gz", "gy"), P("gx", "gz", "gy")),
        check_vma=False,
    )
```

profile of v0, /device:TPU:2, one launch (start us, length us, event | category | flops | bytes accessed | tf_op | source)
XLA Modules:
  0.0 973.8 jit_solution(9382175116959669843)
XLA Ops:
  7.9 170.6 %while.74 = (s32[]{:T(128)}, f32[16,64,128]{1,2,0:T(8,128)}, f32[16,64,128]{1,2,0:T(8,128)}, f32[16,64,128]{1,2,0:T(8,128)}, f32[16,64,128]{1,2,0:T(8,128)}, /*index=5*/s32[]{:T(128)}, f32[4]{0:T(128)S(1)}, f32[4]{0:T(128)S(1)}) while((s32[]{:T(128)}, f32[16,64,128]{1,2,0:T(8,128)}, f32[16,64,128]{1,2,0:T(8,128)}, ...), condition=%wide.region_1.0_spmd.clone, body=%wide.region_0.0_spmd.sunk.clone.sunk | while | flops 3314178 | bytes 9730593 | solution.py:67
  30.5 4.4 collective-permute-start.4
  44.4 6.5 fusion.112
  87.2 6.5 fusion.112
  115.9 5.7 collective-permute-start.4
  131.1 6.5 fusion.112
  172.0 6.5 fusion.112
  204.9 34.8 %reshape.54 = f32[8,2,32,2,64,2]{5,4,3,2,1,0:T(8,128)} reshape(f32[16,64,128]{2,1,0:T(8,128)S(1)} %copy-done.6) | data formatting | bytes 1048576 | tf_op jit(solution)/shard_map/reshape | solution.py:89
  239.8 12.2 %reduce_sum.55 = f32[8,32,64]{2,1,0:T(8,128)S(1)} reduce(f32[8,2,32,2,64,2]{5,4,3,2,1,0:T(8,128)} %reshape.54, f32[]{:T(128)} %constant.215.clone.1), dimensions={1,3,5}, to_apply=%region_3.0 | reduce | flops 114688 | bytes 589828 | tf_op jit(solution)/shard_map/reduce_sum | solution.py:90
  256.7 4.8 fusion.30
  263.0 34.9 %reshape.53 = f32[8,2,32,2,64,2]{5,4,3,2,1,0:T(8,128)} reshape(f32[16,64,128]{2,1,0:T(8,128)S(1)} %copy.49) | data formatting | bytes 1048576 | tf_op jit(solution)/shard_map/reshape | solution.py:89
  297.9 12.2 %reduce_sum.54 = f32[8,32,64]{2,1,0:T(8,128)S(1)} reduce(f32[8,2,32,2,64,2]{5,4,3,2,1,0:T(8,128)} %reshape.53, f32[]{:T(128)} %constant.215.clone.1), dimensions={1,3,5}, to_apply=%region_2.0 | reduce | flops 114688 | bytes 589828 | tf_op jit(solution)/shard_map/reduce_sum | solution.py:90
  310.2 114.2 %while.75 = (s32[]{:T(128)}, f32[8,32,64]{2,1,0:T(8,128)S(1)}, f32[8,32,64]{2,1,0:T(8,128)S(1)}, f32[8,32,64]{2,1,0:T(8,128)S(1)}, f32[8,32,64]{2,1,0:T(8,128)S(...) while((s32[]{:T(128)}, f32[8,32,64]{2,1,0:T(8,128)S(1)}, f32[8,32,64]{2,1,0:T(8,128)S(1)}, ...), condition=%wide.region_5.0_spmd.clone, body=%wide.region_4.0_spmd.sunk.clone.sunk | while | flops 379474 | bytes 1240365 | solution.py:67
  323.3 4.7 collective-permute-done.9
  328.0 4.5 collective-permute-start.10
  352.2 4.7 collective-permute-done.9
  379.8 4.7 collective-permute-done.9
  384.6 4.3 collective-permute-start.10
  435.0 5.7 mul.278
  452.4 5.7 reshape.55
  460.7 103.1 %while.76 = (s32[]{:T(128)}, f32[4,16,32]{2,1,0:T(8,128)S(1)}, f32[4,16,32]{2,1,0:T(8,128)S(1)}, f32[4,16,32]{2,1,0:T(8,128)S(1)}, f32[4,16,32]{2,1,0:T(8,128)S(...) while((s32[]{:T(128)}, f32[4,16,32]{2,1,0:T(8,128)S(1)}, f32[4,16,32]{2,1,0:T(8,128)S(1)}, ...), condition=%wide.region_9.0_spmd.clone, body=%wide.region_8.0_spmd.sunk.clone.sunk | while | flops 47922 | bytes 235437 | solution.py:67
  467.8 4.5 collective-permute-start.14
  474.1 4.3 collective-permute-done.15
  499.2 4.3 collective-permute-done.15
  524.3 4.3 collective-permute-done.15
  549.4 4.3 collective-permute-done.15
  593.6 5.7 collective-permute-done.42
  599.4 356.2 %while.77 = (s32[]{:T(128)}, f32[16,8,16]{2,1,0:T(8,128)S(1)}, f32[16,8,16]{2,1,0:T(8,128)S(1)}, f32[16,8,16]{2,1,0:T(8,128)S(1)}, f32[16,8,16]{2,1,0:T(8,128)S(...) while((s32[]{:T(128)}, f32[16,8,16]{2,1,0:T(8,128)S(1)}, ...), condition=%wide.region_13.14_spmd.clone, body=%wide.region_12.13_spmd.sunk.clone.sunk | while | flops 83042 | bytes 145085 | solution.py:67
  603.3 4.3 collective-permute-done.19
  622.1 4.3 collective-permute-done.19
  640.8 4.3 collective-permute-done.19
  659.5 4.3 collective-permute-done.19
  678.2 4.3 collective-permute-done.19
  696.9 4.3 collective-permute-done.19
  715.6 4.3 collective-permute-done.19
  734.9 4.3 collective-permute-done.19
  753.3 4.3 collective-permute-done.19
  771.7 4.3 collective-permute-done.19
  790.5 4.3 collective-permute-done.19
  809.2 4.3 collective-permute-done.19
  827.9 4.3 collective-permute-done.19
  846.7 4.3 collective-permute-done.19
  865.6 4.7 collective-permute-done.19
  884.1 4.3 collective-permute-done.19
  902.8 4.3 collective-permute-done.19
  921.6 4.3 collective-permute-done.19
  940.8 4.3 collective-permute-done.19
  959.5 4.3 collective-permute-done.44
  (704 shorter events, 686.9 us)
Async XLA Ops:
  30.5 8.2 collective-permute-start.4
  36.2 6.0 collective-permute-start.5
  73.4 7.6 collective-permute-start.4
  78.5 6.4 collective-permute-start.5
  115.9 9.5 collective-permute-start.4
  122.9 6.0 collective-permute-start.5
  158.6 7.7 collective-permute-start.4
  163.8 6.0 collective-permute-start.5
  198.6 53.4 %collective-permute-start.27 = (f32[18,1,130]{2,1,0:T(1,128)}, f32[18,1,130]{2,1,0:T(1,128)}, u32[]{:S(2)}, u32[]{:S(2)}) collective-permute-start(f32[18,1,130]{2,1,0:T(1,128)} %copy.46), channel_id=1, source_target_pairs={{0,1},{1,2},{2,3},{3,4},{4,5},{5,6},{6,7},{8,9},{9,10},{10,11},{11... | collective-permute-start | bytes 28088 | tf_op jit(solution)/shard_map/ppermute | solution.py:25
  203.5 51.0 %collective-permute-start.26 = (f32[18,1,130]{2,1,0:T(1,128)}, f32[18,1,130]{2,1,0:T(1,128)}, u32[]{:S(2)}, u32[]{:S(2)}) collective-permute-start(f32[18,1,130]{2,1,0:T(1,128)} %copy.44), channel_id=1, source_target_pairs={{1,0},{2,1},{3,2},{4,3},{5,4},{6,5},{7,6},{9,8},{10,9},{11,10},{12... | collective-permute-start | bytes 28088 | tf_op jit(solution)/shard_map/ppermute | solution.py:27
  319.3 8.6 collective-permute-start.9
  328.0 7.0 collective-permute-start.10
  348.6 8.3 collective-permute-start.9
  375.9 8.5 collective-permute-start.9
  384.6 6.8 collective-permute-start.10
  404.8 8.3 collective-permute-start.9
  413.3 6.4 collective-permute-start.10
  431.5 11.8 %collective-permute-start.30 = (f32[10,32,1]{2,1,0:T(8,128)S(1)}, f32[10,32,1]{2,1,0:T(8,128)S(1)}, u32[]{:S(2)}, u32[]{:S(2)}) collective-permute-start(f32[10,32,1]{2,1,0:T(8,128)S(1)} %get-tuple-element.742), channel_id=1, source_target_pairs={{0,8},{8,16},{16,24},{1,9},{9,17},{17,25},{2,10},{10,18},{18,26},{... | collective-permute-start | bytes 3848 | tf_op jit(solution)/shard_map/ppermute | solution.py:25
  433.7 9.6 collective-permute-start.31
  467.8 6.3 collective-permute-start.14
  472.3 6.0 collective-permute-start.15
  497.4 6.0 collective-permute-start.15
  522.5 6.0 collective-permute-start.15
  547.7 6.0 collective-permute-start.15
  572.7 6.0 collective-permute-start.37
  601.5 6.2 collective-permute-start.19
  620.2 6.2 collective-permute-start.19
  638.9 6.2 collective-permute-start.19
  657.6 6.2 collective-permute-start.19
  676.3 6.2 collective-permute-start.19
  695.0 6.2 collective-permute-start.19
  713.7 6.2 collective-permute-start.19
  720.0 6.0 collective-permute-start.20
  733.0 6.2 collective-permute-start.19
  751.5 6.2 collective-permute-start.19
  769.9 6.2 collective-permute-start.19
  788.6 6.2 collective-permute-start.19
  807.3 6.2 collective-permute-start.19
  826.1 6.2 collective-permute-start.19
  844.8 6.2 collective-permute-start.19
  863.5 6.8 collective-permute-start.19
  882.2 6.2 collective-permute-start.19
  900.9 6.2 collective-permute-start.19
  919.7 6.2 collective-permute-start.19
  926.0 6.2 collective-permute-start.20
  939.0 6.2 collective-permute-start.19
  957.6 6.2 collective-permute-start.44
  963.9 6.9 collective-permute-start.45
  (152 other events, 804.5 us)
where the time goes:
time: 980 us; the launch traced here: 974 us
  starting transfers between devices  367 us (37%)
  waiting for transfers between devices  303 us (31%)
  local copies, waits for them, and re-layouts  188 us (19%)
  other arithmetic  111 us (11%)
    ppermute x85, waiting for transfers between devices, extended_2(): lax.ppermute(head, axis, [((i + 1) % count, i) for i in range(ends)])  268 us
    ppermute x85, starting transfers between devices, extended_2(): lax.ppermute(tail, axis, [(i, (i + 1) % count) for i in range(ends)])  221 us
    ppermute x85, starting transfers between devices, extended_2(): lax.ppermute(head, axis, [((i + 1) % count, i) for i in range(ends)])  145 us
    reshape x4, local copies, waits for them, and re-layouts, restrict_four(): blocks = field.reshape(first // 2, 2, second // 2, 2, third // 2, 2)  75.7 us
    add x31, other arithmetic, turn(): return (iterate + direction, direction, residual)  67.6 us
    reduce_sum x6, other arithmetic, restrict_four(): return blocks.sum(axis=(1, 3, 5)) * 0.5  29.8 us
    ppermute x85, waiting for transfers between devices, extended_2(): lax.ppermute(tail, axis, [(i, (i + 1) % count) for i in range(ends)])  24.6 us
    dynamic_slice x31, local copies, waits for them, and re-layouts, turn(): first_table[turn_index] * direction + second_table[turn_index] * residual  19.6 us
  transfers between devices with their start and end apart: 173, of which 119 were waited for; matrix products, arithmetic and copies ran while one was open for 11% of the time, Pallas kernels for 0%

commit v1 on v0

v1 whole, which is shorter than its diff:
```python
import jax
import jax.numpy as jnp
from jax import lax
from jax.experimental import pallas as pl
from jax.experimental.pallas import tpu as pltpu
from jax.sharding import PartitionSpec as P

DEGREE = 4
LEVELS = 3
BOTTOM_ITERS = 20

smooth_low = 1.5
smooth_top = 12.0
absorb_top = 1.0
bottom_low = 0.008

F32 = jnp.float32
HALO = 5
GROUPS = 25
LANES = 128


def cheb_tables(count, lower, upper):
    theta = (upper + lower) / 2.0
    delta = (upper - lower) / 2.0
    sigma = theta / delta
    rho_value = 1.0 / sigma
    firsts = []
    seconds = []
    for turn_index in range(count - 1):
        rho_next = 1.0 / (2.0 * sigma - rho_value)
        firsts.append(rho_next * rho_value)
        seconds.append(2.0 * rho_next / delta)
        rho_value = rho_next
    return (1.0 / theta, firsts, seconds)


def shift(value, axis, step):
    count = lax.axis_size(axis)
    return lax.ppermute(value, axis, [(i, (i + step) % count) for i in range(count)])


def flag(condition):
    return jnp.where(condition, 1.0, 0.0).astype(F32)


def edges(axis):
    index = lax.axis_index(axis)
    return flag(index > 0), flag(index < lax.axis_size(axis) - 1)


def lane_iota(rows):
    return lax.broadcasted_iota(jnp.int32, (rows, LANES), 1)


def row_iota(rows):
    return lax.broadcasted_iota(jnp.int32, (rows, LANES), 0)


def pair_sum(out_start, count):
    row = lax.broadcasted_iota(jnp.int32, (LANES, LANES), 0)
    column = lax.broadcasted_iota(jnp.int32, (LANES, LANES), 1) - out_start
    hit = (row // 2 == column) & (column >= 0) & (column < count)
    return jnp.where(hit, 0.5, 0.0).astype(F32)


def exact_dot(a, b):
    return jnp.dot(a, b, preferred_element_type=F32, precision=lax.Precision.HIGHEST)


def call(kernel, outs, scratch, *args):
    result = pl.pallas_call(
        kernel,
        out_shape=[jax.ShapeDtypeStruct(s, F32) for s in outs],
        in_specs=[pl.BlockSpec(memory_space=pltpu.VMEM)] * len(args),
        out_specs=[pl.BlockSpec(memory_space=pltpu.VMEM)] * len(outs),
        scratch_shapes=[pltpu.VMEM(s, F32) for s in scratch],
        compiler_params=pltpu.CompilerParams(vmem_limit_bytes=32 << 20),
    )(*args)
    return result


def step_rows(tiles, coef, sources, plane, start, rows, mask, coefs, b_scale, olds):
    lane = lane_iota(rows)
    here = pl.ds(start, rows)
    values = [t[plane, here, :] for t in tiles]
    right = [pltpu.roll(v, LANES - 1, 1) for v in values]
    left = [pltpu.roll(v, 1, 1) for v in values]
    if len(tiles) == 2:
        right = [
            jnp.where(lane == LANES - 1, right[1], right[0]),
            jnp.where(lane == LANES - 1, right[0], right[1]),
        ]
        left = [jnp.where(lane == 0, left[1], left[0]), jnp.where(lane == 0, left[0], left[1])]
    results = []
    for i, t in enumerate(tiles):
        around = (
            (right[i] + left[i])
            + (t[plane - 1, here, :] + t[plane + 1, here, :])
            + (t[plane, pl.ds(start - 1, rows), :] + t[plane, pl.ds(start + 1, rows), :])
        )
        if mask is not None:
            around = around * mask[i]
        inner = around - coef[i][plane, here, :] * values[i]
        of_value, of_source, of_old = coefs
        out = of_value * values[i] + b_scale * inner
        if of_source:
            out = out + of_source * sources[i][plane, here, :]
        if of_old:
            out = out + of_old * olds[i][plane, here, :]
        results.append(out)
    return results


def smooth(source, coef, bufs, planes, full_x, row_start, rows, masks, plane_ok, level_top, chunk):
    start_scale, firsts, seconds = cheb_tables(DEGREE + 1, smooth_low, level_top)
    now, other = source, None
    for k in range(DEGREE):
        a, b = firsts[k], seconds[k]
        target = bufs[k % 2]
        if k == 0:
            coefs = ((1.0 + a) * start_scale + b, 0.0, 0.0)
            b_here = b * start_scale
        elif k == 1:
            coefs = (1.0 + a, b - a * start_scale, 0.0)
            b_here = b
        else:
            coefs = (1.0 + a, b, -a)
            b_here = b
        low, high = (1, planes - 1) if full_x else (k + 1, planes - 1 - k)

        def body(plane, carry, now=now, target=target, coefs=coefs, b_here=b_here):
            scale = b_here * plane_ok(plane)
            for r in range(row_start, row_start + rows, chunk):
                part = [m[r - row_start : r - row_start + chunk, :] for m in masks]
                out = step_rows(
                    now, coef, source, plane, r, chunk, part, coefs, scale, target
                )
                for t, o in zip(target, out):
                    t[plane, pl.ds(r, chunk), :] = o
            return carry

        lax.fori_loop(low, high, body, 0)
        now = target
    return now


def residual_rows(tiles, coef, source, plane, start, rows):
    t = tiles[0]
    here = pl.ds(start, rows)
    value = t[plane, here, :]
    right = pltpu.roll(value, LANES - 1, 1)
    left = pltpu.roll(value, 1, 1)
    if len(tiles) == 2:
        lane = lane_iota(rows)
        far = tiles[1][plane, here, :]
        right = jnp.where(lane == LANES - 1, pltpu.roll(far, LANES - 1, 1), right)
        left = jnp.where(lane == 0, pltpu.roll(far, 1, 1), left)
    around = (
        (right + left)
        + (t[plane - 1, here, :] + t[plane + 1, here, :])
        + (t[plane, pl.ds(start - 1, rows), :] + t[plane, pl.ds(start + 1, rows), :])
    )
    return source[0][plane, here, :] - coef[0][plane, here, :] * value + around


def clear_pads(ref, planes, first, last):
    for p in range(planes):
        ref[p, 0:first, :] = jnp.zeros((first, LANES), F32)
        ref[p, last : last + 8, :] = jnp.zeros((8, LANES), F32)


S0_PLANES = list(range(1, 25))
C0_PLANES = list(range(2, 24))
STRIPS0 = [("s", p) for p in S0_PLANES] + [("c", p) for p in C0_PLANES]


def plane0(name, p, rs, ab, fl, fr):
    if name == "s":
        if p < 5:
            return fl, p
        if p < 21:
            return rs, p - 5
        return fr, p - 21
    if p < 5:
        return fl, 5 + p - 1
    if p < 21:
        return ab, p - 5
    return fr, 5 + p - 21


def z_strips_kernel(rs, ab, fl, fr, low, high):
    for i, (name, p) in enumerate(STRIPS0):
        ref, q = plane0(name, p, rs, ab, fl, fr)
        low[5 * i : 5 * i + 5, :] = ref[q, 0:5, :]
        high[5 * i : 5 * i + 5, :] = ref[q, 59:64, :]


def pack_lanes(strips, get, low, high, rows):
    lane = lane_iota(rows)
    for t in range((len(strips) + GROUPS - 1) // GROUPS):
        low_tile = jnp.zeros((rows, LANES), F32)
        high_tile = jnp.zeros((rows, LANES), F32)
        for g in range(GROUPS):
            i = t * GROUPS + g
            if i >= len(strips):
                break
            value, base, width = get(*strips[i])
            inside = (lane >= 5 * g) & (lane < 5 * g + 5)
            to_low = (5 * g - base) % LANES
            to_high = (5 * g - (base + width - 5)) % LANES
            a = pltpu.roll(value, to_low, 1) if to_low else value
            b = pltpu.roll(value, to_high, 1) if to_high else value
            low_tile = jnp.where(inside, a, low_tile)
            high_tile = jnp.where(inside, b, high_tile)
        low[t, :, :] = low_tile
        high[t, :, :] = high_tile


def build0_kernel(rs, ab, fl, fr, zl, zh, es, ec, low, high, c1, tmp, gathered):
    x_low, x_high = edges("gx")
    z_low, z_high = edges("gz")
    zero = jnp.zeros((16, LANES), F32)
    for p in range(26):
        ref, q = plane0("s", p, rs, ab, fl, fr)
        scale = x_low if p < 5 else (x_high if p > 20 else None)
        value = ref[q, :, :]
        es[p, 16:80, :] = value if scale is None else value * scale
        es[p, 0:16, :] = zero
        es[p, 80:96, :] = zero
        if p in S0_PLANES:
            i = STRIPS0.index(("s", p))
            below, above = zl[5 * i : 5 * i + 5, :], zh[5 * i : 5 * i + 5, :]
            below, above = below * z_low, above * z_high
            if scale is not None:
                below, above = below * scale, above * scale
            es[p, 11:16, :] = below
            es[p, 80:85, :] = above
    for p in range(26):
        if p in (0, 25):
            continue
        ref, q = plane0("c", p, rs, ab, fl, fr)
        ec[p, 16:80, :] = ref[q, :, :] + 6.0
        ec[p, 0:16, :] = zero
        ec[p, 80:96, :] = zero
        if p in C0_PLANES:
            i = STRIPS0.index(("c", p))
            ec[p, 11:16, :] = zl[5 * i : 5 * i + 5, :] + 6.0
            ec[p, 80:85, :] = zh[5 * i : 5 * i + 5, :] + 6.0

    def get(name, p):
        return (es if name == "s" else ec)[p, 8:88, :], 0, LANES

    pack_lanes(STRIPS0, get, low, high, 80)
    for i in range(8):
        tmp[...] = ab[2 * i, :, :] + ab[2 * i + 1, :, :]
        gathered[32 * i : 32 * i + 32, :] = (
            tmp[pl.ds(0, 32, stride=2), :] + tmp[pl.ds(1, 32, stride=2), :]
        )
    folded = exact_dot(gathered[...], pair_sum(64, 64))
    c1[...] = folded.reshape(8, 32, LANES)


def level0_kernel(es, ec, yl, yh, c1, it0, sc1, s1, cc1, a0, a1, b0, b1, tmp, gathered):
    x_low, x_high = edges("gx")
    y_low, y_high = edges("gy")
    z_low, z_high = edges("gz")
    lane = lane_iota(80)
    row = row_iota(80)
    ok_rows = jnp.where(row < 8, z_low, jnp.where(row >= 72, z_high, 1.0))
    ok_lanes = jnp.where(lane < 64, y_high, y_low)
    for ref, strips in ((s1, S0_PLANES), (cc1, C0_PLANES)):
        name = "s" if ref is s1 else "c"
        for p in range(26):
            if p not in strips:
                if ref is s1 or p not in (0, 25):
                    ref[p, :, :] = jnp.zeros((96, LANES), F32)
                continue
            i = STRIPS0.index((name, p))
            t, g = i // GROUPS, i % GROUPS
            from_low = pltpu.roll(yl[t, :, :], 123 - 5 * g, 1)
            from_high = pltpu.roll(yh[t, :, :], (LANES - 5 * g) % LANES, 1) if g else yh[t, :, :]
            value = jnp.where(lane < 5, from_high, jnp.where(lane >= 123, from_low, 0.0))
            if ref is s1:
                value = value * ok_lanes
            ref[p, 8:88, :] = value
            ref[p, 0:8, :] = jnp.zeros((8, LANES), F32)
            ref[p, 88:96, :] = jnp.zeros((8, LANES), F32)
    for ref in (a0, a1, b0, b1):
        clear_pads(ref, 26, 8, 88)

    def plane_ok(p):
        return jnp.where(p < 5, x_low, jnp.where(p > 20, x_high, 1.0))

    masks = [ok_rows, ok_rows * ok_lanes]
    last = smooth(
        [es, s1], [ec, cc1], [[a0, a1], [b0, b1]], 26, False, 8, 80, masks, plane_ok,
        smooth_top + absorb_top, 16,
    )

    def finish(i, carry):
        for half in range(2):
            p = 5 + 2 * i + half
            for r in range(16, 80, 16):
                it0[2 * i + half, r - 16 : r, :] = last[0][p, r : r + 16, :]
                value = residual_rows(last, [ec], [es], p, r, 16)
                if half == 0:
                    tmp[r - 16 : r, :] = value
                else:
                    tmp[r - 16 : r, :] = tmp[r - 16 : r, :] + value
        start = pl.multiple_of(32 * i, 32)
        gathered[pl.ds(start, 32), :] = (
            tmp[pl.ds(0, 32, stride=2), :] + tmp[pl.ds(1, 32, stride=2), :]
        )
        return carry

    lax.fori_loop(0, 8, finish, 0)
    folded = exact_dot(gathered[...], pair_sum(0, 64))
    sc1[...] = folded.reshape(8, 32, LANES) + c1[...]


STRIPS1 = [("s", p) for p in range(1, 17)] + [("c", p) for p in range(2, 16)]


def build1_kernel(sc, fl, fr, zl, zh, ext, low, high):
    for p in range(18):
        ref, q = (fl, p) if p < 5 else ((sc, p - 5) if p < 13 else (fr, p - 13))
        ext[p, 0:8, :] = zl[p, :, :]
        ext[p, 8:40, :] = ref[q, :, :]
        ext[p, 40:48, :] = zh[p, :, :]

    def get(name, p):
        return ext[p, :, :], (0 if name == "s" else 64), 64

    pack_lanes(STRIPS1, get, low, high, 48)


def level1_kernel(ext, yl, yh, it1, sc2, es, ec, a, b, tmp, gathered):
    x_low, x_high = edges("gx")
    y_low, y_high = edges("gy")
    z_low, z_high = edges("gz")
    lane = lane_iota(48)
    row = row_iota(48)
    ok_rows = jnp.where(row < 8, z_low, jnp.where(row >= 40, z_high, 1.0))
    ok_lanes = jnp.where(lane < 64, 1.0, jnp.where(lane < 96, y_high, y_low))
    ok = ok_rows * ok_lanes
    for p in range(18):
        value = ext[p, :, :]
        for name, ref in (("s", es), ("c", ec)):
            mine = value if name == "s" else pltpu.roll(value, 64, 1)
            if (name, p) in STRIPS1:
                i = STRIPS1.index((name, p))
                t, g = i // GROUPS, i % GROUPS
                from_low = pltpu.roll(yl[t, :, :], 123 - 5 * g, 1)
                from_high = pltpu.roll(yh[t, :, :], (64 - 5 * g) % LANES, 1)
                halo = jnp.where(
                    lane < 69, from_high, jnp.where(lane >= 123, from_low, 0.0)
                )
            else:
                halo = jnp.zeros((48, LANES), F32)
            full = jnp.where(lane < 64, mine, halo)
            if name == "s":
                full = full * ok
                if p < 5:
                    full = full * x_low
                if p > 12:
                    full = full * x_high
            else:
                full = full + 6.0
            ref[p, 8:56, :] = full
    clear_pads(es, 18, 8, 56)
    clear_pads(a, 18, 8, 56)
    clear_pads(b, 18, 8, 56)

    def plane_ok(p):
        return jnp.where(p < 5, x_low, jnp.where(p > 12, x_high, 1.0))

    last = smooth(
        [es], [ec], [[a], [b]], 18, False, 8, 48, [ok], plane_ok,
        smooth_top + 4.0 * absorb_top, 48,
    )
    for i in range(4):
        total = jnp.zeros((32, LANES), F32)
        for half in range(2):
            p = 5 + 2 * i + half
            it1[2 * i + half, :, :] = last[0][p, 16:48, :][:, 0:64]
            total = total + residual_rows(last, [ec], [es], p, 16, 32)
        tmp[...] = total
        gathered[16 * i : 16 * i + 16, :] = (
            tmp[pl.ds(0, 16, stride=2), :] + tmp[pl.ds(1, 16, stride=2), :]
        )
        tmp[...] = ext[5 + 2 * i, 8:40, :] + ext[6 + 2 * i, 8:40, :]
        gathered[64 + 16 * i : 80 + 16 * i, :] = (
            tmp[pl.ds(0, 16, stride=2), :] + tmp[pl.ds(1, 16, stride=2), :]
        )
    lane16 = lane_iota(16)
    folded = exact_dot(gathered[...], pair_sum(0, 64))
    for kind in range(2):
        total = jnp.zeros((16, LANES), F32)
        for i in range(4):
            value = folded[64 * kind + 16 * i : 64 * kind + 16 * i + 16, :]
            amount = (32 * i - 32 * kind) % LANES
            value = pltpu.roll(value, amount, 1) if amount else value
            total = jnp.where(lane16 // 32 == i, value, total)
        sc2[kind, :, :] = total


def level2_kernel(p0, p1, p2, p3, it2, piece, es, ec, a, b, tmp, gathered):
    gx = lax.axis_index("gx")
    y_low, y_high = edges("gy")
    z_low, z_high = edges("gz")
    chip, core = gx // 2, gx % 2
    lane = lane_iota(32)
    row = row_iota(32)
    ok_rows = jnp.where(row < 8, z_low, jnp.where(row >= 24, z_high, 1.0))
    ok_lanes = jnp.where(lane < 32, 1.0, jnp.where(lane < 80, y_high, y_low))
    ok = ok_rows * ok_lanes
    for ref in (es, a, b):
        for p in (0, 33):
            ref[p, :, :] = jnp.zeros((48, LANES), F32)
        clear_pads(ref, 34, 8, 40)
    for k, pieces in enumerate((p0, p1, p2, p3)):
        for j in range(2):
            owner = 2 * ((chip - k + 4) % 4) + (core + j) % 2
            for kind, ref in enumerate((es, ec)):
                mine = pieces[j, kind, :, :]
                halo = pieces[j, 2 + kind, :, :]
                for x in range(4):
                    first = pltpu.roll(mine, (LANES - 32 * x) % LANES, 1) if x else mine
                    above = pltpu.roll(halo, (32 - 32 * x) % LANES, 1) if x != 1 else halo
                    below = pltpu.roll(halo, (96 - 32 * x) % LANES, 1) if x != 3 else halo
                    full = jnp.where(
                        lane < 32,
                        first,
                        jnp.where(lane < 37, above, jnp.where(lane >= 123, below, 0.0)),
                    )
                    if kind == 0:
                        full = full * ok
                    ref[1 + 4 * owner + x, 8:40, :] = full if kind == 0 else full + 6.0
                if kind == 1:
                    total = mine[8:24, :] + pltpu.roll(mine[8:24, :], 96, 1)
                    tmp[...] = total
                    rows = tmp[pl.ds(0, 8, stride=2), :] + tmp[pl.ds(1, 8, stride=2), :]
                    at = pl.multiple_of(128 + 16 * owner, 16)
                    gathered[pl.ds(at, 8), :] = rows
                    gathered[pl.ds(at + 8, 8), :] = pltpu.roll(rows, 64, 1)

    last = smooth(
        [es], [ec], [[a], [b]], 34, True, 8, 32, [ok], lambda p: 1.0,
        smooth_top + 16.0 * absorb_top, 32,
    )
    for x in range(4):
        it2[x, :, :] = last[0][1 + 4 * gx + x, 16:32, :]

    def finish(i, carry):
        total = residual_rows(last, [ec], [es], 1 + 2 * i, 16, 16)
        total = total + residual_rows(last, [ec], [es], 2 + 2 * i, 16, 16)
        tmp[...] = total
        at = pl.multiple_of(8 * i, 8)
        gathered[pl.ds(at, 8), :] = (
            tmp[pl.ds(0, 8, stride=2), :] + tmp[pl.ds(1, 8, stride=2), :]
        )
        return carry

    lax.fori_loop(0, 16, finish, 0)
    lane8 = lane_iota(8)
    folded = exact_dot(gathered[...], pair_sum(0, 16))
    for kind in range(2):
        for half in range(2):
            total = jnp.zeros((8, LANES), F32)
            for x in range(8):
                at = 128 * kind + 8 * (8 * half + x)
                value = folded[at : at + 8, :]
                value = pltpu.roll(value, 16 * x, 1) if x else value
                total = jnp.where(lane8 // 16 == x, value, total)
            piece[kind, half, :, :] = total


def bottom_kernel(g0, g1, g2, g3, it2, out, s, c, a, b, window):
    gx, gy, gz = lax.axis_index("gx"), lax.axis_index("gy"), lax.axis_index("gz")
    lane8 = lane_iota(8)
    lane = lane_iota(64)
    for ref in (s, c, a, b):
        clear_pads(ref, 10, 8, 72)

    def unpack(slot, carry):
        z_owner = (gz - slot + 8) % 8
        at = pl.multiple_of(8 + 8 * z_owner, 8)
        for kind, ref in enumerate((s, c)):
            for x in range(8):
                total = jnp.zeros((8, LANES), F32)
                for m, pieces in enumerate((g0, g1, g2, g3)):
                    y_owner = (gy - m + 4) % 4
                    for half in range(2):
                        value = pieces[slot, kind, half, :, :]
                        start = 64 * half + 16 * y_owner
                        value = pltpu.roll(value, (start - 16 * x + LANES) % LANES, 1)
                        total = jnp.where(lane8 // 16 == 4 * half + y_owner, value, total)
                ref[1 + x, pl.ds(at, 8), :] = total if kind == 0 else total + 6.0
        return carry

    lax.fori_loop(0, 8, unpack, 0)
    zero = jnp.zeros((64, LANES), F32)

    def wrap(ref):
        ref[0, 8:72, :] = jnp.where(lane >= 64, pltpu.roll(ref[8, 8:72, :], 64, 1), 0.0)
        ref[9, 8:72, :] = jnp.where(lane < 64, pltpu.roll(ref[1, 8:72, :], 64, 1), 0.0)

    top = smooth_top + 4.0**LEVELS * absorb_top
    start_scale, firsts, seconds = cheb_tables(BOTTOM_ITERS, bottom_low, top)
    keep_right = jnp.where(lane % 64 == 63, 0.0, 1.0)
    keep_left = jnp.where(lane % 64 == 0, 0.0, 1.0)

    def update(now, target, of_value, of_source, of_old, scale):
        wrap(now)
        for p in range(1, 9):
            value = now[p, 8:72, :]
            around = (
                pltpu.roll(value, LANES - 1, 1) * keep_right
                + pltpu.roll(value, 1, 1) * keep_left
                + (now[p - 1, 8:72, :] + now[p + 1, 8:72, :])
                + (now[p, 7:71, :] + now[p, 9:73, :])
            )
            new = of_value * value + scale * (around - c[p, 8:72, :] * value)
            if of_source is not None:
                new = new + of_source * s[p, 8:72, :]
            if of_old is not None:
                new = new + of_old * target[p, 8:72, :]
            target[p, 8:72, :] = new

    f, g = firsts, seconds
    update(s, a, (1.0 + f[0]) * start_scale + g[0], None, None, g[0] * start_scale)
    update(a, b, 1.0 + f[1], g[1] - f[1] * start_scale, None, g[1])
    bufs = [a, b]
    for k in range(2, BOTTOM_ITERS - 1):
        update(bufs[(k + 1) % 2], bufs[k % 2], 1.0 + f[k], g[k], -f[k], g[k])
    last = bufs[(BOTTOM_ITERS - 2) % 2]
    row24 = row_iota(24)
    lane24 = lane_iota(24)
    low_row = pl.multiple_of(8 * gz, 8)
    rows_ok = ((row24 >= 8) | (gz > 0)) & ((row24 < 16) | (gz < 7))
    lanes_ok = ((lane24 >= 1) | (gy > 0)) & ((lane24 <= 16) | (gy < 3)) & (lane24 < 18)
    row = lax.broadcasted_iota(jnp.int32, (LANES, LANES), 0)
    column = lax.broadcasted_iota(jnp.int32, (LANES, LANES), 1)
    center = column // 2 + 1
    side = jnp.where(column % 2 == 0, center - 1, center + 1)
    spread = jnp.where(row == center, 0.75, jnp.where(row == side, 0.25, 0.0))
    spread = jnp.where(column < 32, spread, 0.0).astype(F32)
    for j in range(4):
        x = 2 * gx - 1 + j
        x_ok = (x >= 0) & (x < 16)
        xc = jnp.clip(x, 0, 15)
        value = last[1 + xc % 8, pl.ds(low_row, 24), :]
        amount = (2 * LANES - 64 * (xc // 8) - 16 * gy + 1) % LANES
        value = pltpu.roll(value, amount, 1)
        value = jnp.where(rows_ok & lanes_ok & x_ok, value, 0.0)
        window[24 * j : 24 * j + 24, :] = value
    wide = exact_dot(window[...], spread)
    planes = [wide[24 * j : 24 * j + 24, :] for j in range(4)]
    for i in range(4):
        base = i // 2 + 1
        near = base - 1 if i % 2 == 0 else base + 1
        mixed = 0.75 * planes[base] + 0.25 * planes[near]
        window[0:24, :] = mixed
        even = 0.75 * window[8:16, :] + 0.25 * window[7:15, :]
        odd = 0.75 * window[8:16, :] + 0.25 * window[9:17, :]
        window[pl.ds(32, 8, stride=2), :] = even
        window[pl.ds(33, 8, stride=2), :] = odd
        out[i, :, :] = (it2[i, :, :] + window[32:48, :])[:, 0:32]


def exchange(low, high, axis):
    return shift(high, axis, 1), shift(low, axis, -1)


def on_device(rs, ab):
    fl, fr = exchange(
        jnp.concatenate((rs[:5], ab[:4])), jnp.concatenate((rs[11:], ab[12:])), "gx"
    )
    low, high = call(z_strips_kernel, [(230, LANES)] * 2, [], rs, ab, fl, fr)
    zl, zh = exchange(low, high, "gz")
    es, ec, low, high, c1 = call(
        build0_kernel,
        [(26, 96, LANES)] * 2 + [(2, 80, LANES)] * 2 + [(8, 32, LANES)],
        [(64, LANES), (256, LANES)],
        rs, ab, fl, fr, zl, zh,
    )
    yl, yh = exchange(low, high, "gy")
    it0, sc1 = call(
        level0_kernel,
        [(16, 64, LANES), (8, 32, LANES)],
        [(26, 96, LANES)] * 6 + [(64, LANES), (256, LANES)],
        es, ec, yl, yh, c1,
    )
    fl, fr = exchange(sc1[:5], sc1[3:], "gx")
    ext = jnp.concatenate((fl, sc1, fr))
    zl, zh = exchange(ext[:, :8], ext[:, 24:], "gz")
    ext, low, high = call(
        build1_kernel,
        [(18, 48, LANES)] + [(2, 48, LANES)] * 2,
        [],
        sc1, fl, fr, zl, zh,
    )
    yl, yh = exchange(low, high, "gy")
    it1, sc2 = call(
        level1_kernel,
        [(8, 32, 64), (2, 16, LANES)],
        [(18, 64, LANES)] * 4 + [(32, LANES), (128, LANES)],
        ext, yl, yh,
    )
    zl, zh = exchange(sc2[:, :8], sc2[:, 8:], "gz")
    mine = jnp.concatenate((zl, sc2, zh), axis=1)
    yl, yh = exchange(mine, mine, "gy")
    part = lax.broadcasted_iota(jnp.int32, mine.shape, 2) % 32
    halo = jnp.where(part < 16, yh, yl)
    mine = jnp.concatenate((mine, halo))
    partner = lax.ppermute(mine, "gx", [(i, i ^ 1) for i in range(8)])
    pair = jnp.stack((mine, partner))
    pairs = [pair] + [shift(pair, "gx", 2 * k) for k in range(1, 4)]
    it2, piece = call(
        level2_kernel,
        [(4, 16, LANES), (2, 2, 8, LANES)],
        [(34, 48, LANES)] * 4 + [(16, LANES), (256, LANES)],
        *pairs,
    )
    column = jnp.stack([piece] + [shift(piece, "gz", k) for k in range(1, 8)])
    grids = [column] + [shift(column, "gy", k) for k in range(1, 4)]
    (corrected,) = call(
        bottom_kernel,
        [(4, 16, 32)],
        [(10, 80, LANES)] * 4 + [(96, LANES)],
        *grids, it2,
    )
    return it0, it1, corrected


def solution(mesh):
    placed = (P("gx", "gz", "gy"), P("gx", "gz", "gy"))
    return jax.shard_map(
        on_device,
        mesh=mesh,
        in_specs=placed,
        out_specs=(P("gx", "gz", "gy"), P("gx", "gz", "gy"), P("gx", "gz", "gy")),
        check_vma=False,
    )
```

time: 980 us -> 136 us (0.14)
  starting transfers between devices: 367 us -> 48.5 us
  waiting for transfers between devices: 303 us -> 41.6 us
  local copies, waits for them, and re-layouts: 188 us -> 2.18 us
  other arithmetic: 111 us -> 0.08 us
  Pallas kernels: 0 us -> 42.2 us
    ppermute x173 -> x30, starting transfers between devices: 367 us -> 48.5 us  [the longest x29 48.4 us: shift(): lax.ppermute(value, axis, [(i, (i + step) % count) for i in range(count)])]
    ppermute x173 -> x30, waiting for transfers between devices: 303 us -> 41.6 us  [the longest x29 40.4 us: shift(): lax.ppermute(value, axis, [(i, (i + step) % count) for i in range(count)])]
    reshape x4 -> x0, local copies, waits for them, and re-layouts: 75.7 us -> none  [restrict_four(): blocks = field.reshape(first // 2, 2, second // 2, 2, third // 2, 2)]
    add x32 -> x0, other arithmetic: 67.6 us -> none  [the longest x31 67.6 us: turn(): return (iterate + direction, direction, residual)]
    pallas_call x0 -> x7, Pallas kernels: none -> 42.2 us  [call(): pl.pallas_call(kernel, out_shape=[jax.ShapeDtypeStruct(s, F32) for s in o...]
    dynamic_slice x62 -> x0, local copies, waits for them, and re-layouts: 38 us -> none  [the longest x31 19.6 us: turn(): first_table[turn_index] * direction + second_table[turn_index] * residual]
    reduce_sum x6 -> x0, other arithmetic: 29.8 us -> none  [restrict_four(): return blocks.sum(axis=(1, 3, 5)) * 0.5]
    slice x65 -> x5, local copies, waits for them, and re-layouts: 30.1 us -> 2.12 us  [the longest x1 1.1 us: on_device(): rs[:5]]
  transfers between devices with their start and end apart: 173 -> 30, of which waited for: 119 -> 20; matrix products, arithmetic and copies ran while one was open for 11% -> 0% of each run, Pallas kernels for 0% -> 0%
where the time goes in v1:
time: 136 us; the launch traced here: 135 us
  starting transfers between devices  48.5 us (36%)
  Pallas kernels  42.2 us (31%)
  waiting for transfers between devices  41.6 us (31%)
  local copies, waits for them, and re-layouts  2.18 us (2%)
    ppermute x29, starting transfers between devices, shift(): lax.ppermute(value, axis, [(i, (i + step) % count) for i in range(count)])  48.4 us
    pallas_call x7, Pallas kernels, call(): pl.pallas_call(kernel, out_shape=[jax.ShapeDtypeStruct(s, F32) for s in o...  42.2 us
    ppermute x29, waiting for transfers between devices, shift(): lax.ppermute(value, axis, [(i, (i + step) % count) for i in range(count)])  40.4 us
  transfers between devices with their start and end apart: 30, of which 20 were waited for; matrix products, arithmetic and copies ran while one was open for 0% of the time, Pallas kernels for 0%

profile of v1, /device:TPU:2, one launch (start us, length us, event | category | flops | bytes accessed | tf_op | source)
XLA Modules:
  0.0 135.4 jit_solution(14602002633541898801)
XLA Ops:
  0.7 1.1 fusion.2
  1.8 1.0 fusion.3
  2.8 1.7 %collective-permute-start.1 = (f32[9,64,128]{2,1,0:T(8,128)S(1)}, f32[9,64,128]{2,1,0:T(8,128)S(1)}, u32[]{:S(2)}, u32[]{:S(2)}) collective-permute-start(f32[9,64,128]{2,1,0:T(8,128)S(1)} %pad_maximum_fusion.1), channel_id=1, source_target_pairs={{0,224},{32,0},{64,32},{96,64},{128,96},{160,128},{192,160},{224,1... | collective-permute-start | bytes 884744 | tf_op jit(solution)/shard_map/ppermute | solution.py:40
  4.6 4.4 %collective-permute-done.fl = f32[9,64,128]{2,1,0:T(8,128)S(1)} collective-permute-done((f32[9,64,128]{2,1,0:T(8,128)S(1)}, f32[9,64,128]{2,1,0:T(8,128)S(1)}, u32[]{:S(2)}, u32[]{:S(2)}) %collective-permute-start) | collective-permute-done | bytes 294944 | tf_op jit(solution)/shard_map/ppermute | solution.py:40
  9.0 2.0 %collective-permute-start.2 = (f32[230,128]{1,0:T(8,128)S(1)}, f32[230,128]{1,0:T(8,128)S(1)}, u32[]{:S(2)}, u32[]{:S(2)}) collective-permute-start(f32[230,128]{1,0:T(8,128)S(1)} %get-tuple-element.19), channel_id=1, source_target_pairs={{0,1},{1,2},{2,3},{3,4},{4,5},{5,6},{6,7},{7,0},{8,9},{9,10},{10,1... | collective-permute-start | bytes 353288 | tf_op jit(solution)/shard_map/ppermute | solution.py:40
  11.0 4.0 %collective-permute-start.3 = (f32[230,128]{1,0:T(8,128)S(1)}, f32[230,128]{1,0:T(8,128)S(1)}, u32[]{:S(2)}, u32[]{:S(2)}) collective-permute-start(f32[230,128]{1,0:T(8,128)S(1)} %get-tuple-element.20), channel_id=1, source_target_pairs={{0,7},{1,0},{2,1},{3,2},{4,3},{5,4},{6,5},{7,6},{8,15},{9,8},{10,9... | collective-permute-start | bytes 353288 | tf_op jit(solution)/shard_map/ppermute | solution.py:40
  15.0 3.1 %collective-permute-done.2.zl = f32[230,128]{1,0:T(8,128)S(1)} collective-permute-done((f32[230,128]{1,0:T(8,128)S(1)}, f32[230,128]{1,0:T(8,128)S(1)}, u32[]{:S(2)}, u32[]{:S(2)}) %collective-permute-start.2) | collective-permute-done | bytes 117792 | tf_op jit(solution)/shard_map/ppermute | solution.py:40
  18.1 1.2 shard_map.50
  19.2 1.7 %collective-permute-start.4 = (f32[2,80,128]{2,1,0:T(8,128)S(1)}, f32[2,80,128]{2,1,0:T(8,128)S(1)}, u32[]{:S(2)}, u32[]{:S(2)}) collective-permute-start(f32[2,80,128]{2,1,0:T(8,128)S(1)} %get-tuple-element.23), channel_id=1, source_target_pairs={{0,8},{8,16},{16,24},{24,0},{1,9},{9,17},{17,25},{25,1},{2,10},{10... | collective-permute-start | bytes 245768 | tf_op jit(solution)/shard_map/ppermute | solution.py:40
  20.9 1.7 %collective-permute-start.5 = (f32[2,80,128]{2,1,0:T(8,128)S(1)}, f32[2,80,128]{2,1,0:T(8,128)S(1)}, u32[]{:S(2)}, u32[]{:S(2)}) collective-permute-start(f32[2,80,128]{2,1,0:T(8,128)S(1)} %get-tuple-element.24), channel_id=1, source_target_pairs={{0,24},{8,0},{16,8},{24,16},{1,25},{9,1},{17,9},{25,17},{2,26},{10... | collective-permute-start | bytes 245768 | tf_op jit(solution)/shard_map/ppermute | solution.py:40
  22.5 3.1 %collective-permute-done.4.yl = f32[2,80,128]{2,1,0:T(8,128)S(1)} collective-permute-done((f32[2,80,128]{2,1,0:T(8,128)S(1)}, f32[2,80,128]{2,1,0:T(8,128)S(1)}, u32[]{:S(2)}, u32[]{:S(2)}) %collective-permute-start.4) | collective-permute-done | bytes 81952 | tf_op jit(solution)/shard_map/ppermute | solution.py:40
  25.7 13.3 %shard_map.51 = (f32[16,64,128]{2,1,0:T(8,128)}, f32[8,32,128]{2,1,0:T(8,128)S(1)}) custom-call(f32[26,96,128]{2,1,0:T(8,128)S(1)} %get-tuple-element.21.es, f32[26,96,128]{2,1,0:T(8,128)S(1)} %get-tuple-element.22.ec, f32[2,80,128]{2,1,0:T(8,128)S(1)} %collective-permute-done.4.yl, f32[2,80,128]{2,1,0:T(8,128)S(1)} %collective-permute-done.5.yh, ...), custom_call_target="tpu_custom_call" | custom-call | tf_op jit(solution)/shard_map/pallas_call | solution.py:72
  39.0 1.7 %collective-permute-start.7 = (f32[5,32,128]{2,1,0:T(8,128)S(1)}, f32[5,32,128]{2,1,0:T(8,128)S(1)}, u32[]{:S(2)}, u32[]{:S(2)}) collective-permute-start(f32[5,32,128]{2,1,0:T(8,128)S(1)} %get-tuple-element.41), channel_id=1, source_target_pairs={{0,224},{32,0},{64,32},{96,64},{128,96},{160,128},{192,160},{224,1... | collective-permute-start | bytes 245768 | tf_op jit(solution)/shard_map/ppermute | solution.py:40
  40.7 2.1 %collective-permute-done.6.fl = f32[5,32,128]{2,1,0:T(8,128)S(1)} collective-permute-done((f32[5,32,128]{2,1,0:T(8,128)S(1)}, f32[5,32,128]{2,1,0:T(8,128)S(1)}, u32[]{:S(2)}, u32[]{:S(2)}) %collective-permute-start.6) | collective-permute-done | bytes 81952 | tf_op jit(solution)/shard_map/ppermute | solution.py:40
  43.0 3.4 %collective-permute-start.9 = (f32[18,8,128]{2,1,0:T(8,128)S(1)}, f32[18,8,128]{2,1,0:T(8,128)S(1)}, u32[]{:S(2)}, u32[]{:S(2)}) collective-permute-start(f32[18,8,128]{2,1,0:T(8,128)S(1)} %get-tuple-element.39), channel_id=1, source_target_pairs={{0,7},{1,0},{2,1},{3,2},{4,3},{5,4},{6,5},{7,6},{8,15},{9,8},{10,9... | collective-permute-start | bytes 221192 | tf_op jit(solution)/shard_map/ppermute | solution.py:40
  46.4 2.2 %collective-permute-done.8.zl = f32[18,8,128]{2,1,0:T(8,128)S(1)} collective-permute-done((f32[18,8,128]{2,1,0:T(8,128)S(1)}, f32[18,8,128]{2,1,0:T(8,128)S(1)}, u32[]{:S(2)}, u32[]{:S(2)}) %collective-permute-start.8) | collective-permute-done | bytes 73760 | tf_op jit(solution)/shard_map/ppermute | solution.py:40
  49.1 1.7 %collective-permute-start.10 = (f32[2,48,128]{2,1,0:T(8,128)S(1)}, f32[2,48,128]{2,1,0:T(8,128)S(1)}, u32[]{:S(2)}, u32[]{:S(2)}) collective-permute-start(f32[2,48,128]{2,1,0:T(8,128)S(1)} %get-tuple-element.29), channel_id=1, source_target_pairs={{0,8},{8,16},{16,24},{24,0},{1,9},{9,17},{17,25},{25,1},{2,10},{10... | collective-permute-start | bytes 147464 | tf_op jit(solution)/shard_map/ppermute | solution.py:40
  50.8 1.7 %collective-permute-start.11 = (f32[2,48,128]{2,1,0:T(8,128)S(1)}, f32[2,48,128]{2,1,0:T(8,128)S(1)}, u32[]{:S(2)}, u32[]{:S(2)}) collective-permute-start(f32[2,48,128]{2,1,0:T(8,128)S(1)} %get-tuple-element.30), channel_id=1, source_target_pairs={{0,24},{8,0},{16,8},{24,16},{1,25},{9,1},{17,9},{25,17},{2,26},{10... | collective-permute-start | bytes 147464 | tf_op jit(solution)/shard_map/ppermute | solution.py:40
  52.4 2.5 %collective-permute-done.10.yl = f32[2,48,128]{2,1,0:T(8,128)S(1)} collective-permute-done((f32[2,48,128]{2,1,0:T(8,128)S(1)}, f32[2,48,128]{2,1,0:T(8,128)S(1)}, u32[]{:S(2)}, u32[]{:S(2)}) %collective-permute-start.10) | collective-permute-done | bytes 49184 | tf_op jit(solution)/shard_map/ppermute | solution.py:40
  55.0 6.2 %shard_map.53 = (f32[8,32,64]{2,1,0:T(8,128)}, f32[2,16,128]{2,1,0:T(8,128)S(1)}) custom-call(f32[18,48,128]{2,1,0:T(8,128)S(1)} %get-tuple-element.28.ext, f32[2,48,128]{2,1,0:T(8,128)S(1)} %collective-permute-done.10.yl, f32[2,48,128]{2,1,0:T(8,128)S(1)} %collective-permute-done.11.yh), custom_call_target="tpu_custom_call" | custom-call | tf_op jit(solution)/shard_map/pallas_call | solution.py:72
  61.2 2.9 %collective-permute-start.12 = (f32[2,8,128]{2,1,0:T(8,128)S(1)}, f32[2,8,128]{2,1,0:T(8,128)S(1)}, u32[]{:S(2)}, u32[]{:S(2)}) collective-permute-start(f32[2,8,128]{2,1,0:T(8,128)S(1)} %get-tuple-element.46), channel_id=1, source_target_pairs={{0,1},{1,2},{2,3},{3,4},{4,5},{5,6},{6,7},{7,0},{8,9},{9,10},{10,1... | collective-permute-start | bytes 24584 | tf_op jit(solution)/shard_map/ppermute | solution.py:40
  64.5 1.6 %collective-permute-done.12 = f32[2,8,128]{2,1,0:T(8,128)S(1)} collective-permute-done((f32[2,8,128]{2,1,0:T(8,128)S(1)}, f32[2,8,128]{2,1,0:T(8,128)S(1)}, u32[]{:S(2)}, u32[]{:S(2)}) %collective-permute-start.12) | collective-permute-done | bytes 8224 | tf_op jit(solution)/shard_map/ppermute | solution.py:40
  66.1 1.9 %collective-permute-done.13 = f32[2,8,128]{2,1,0:T(8,128)S(1)} collective-permute-done((f32[2,8,128]{2,1,0:T(8,128)S(1)}, f32[2,8,128]{2,1,0:T(8,128)S(1)}, u32[]{:S(2)}, u32[]{:S(2)}) %collective-permute-start.13) | collective-permute-done | bytes 8224 | tf_op jit(solution)/shard_map/ppermute | solution.py:40
  68.0 2.9 %collective-permute-start.14 = (f32[2,32,128]{2,1,0:T(8,128)S(1)}, f32[2,32,128]{2,1,0:T(8,128)S(1)}, u32[]{:S(2)}, u32[]{:S(2)}) collective-permute-start(f32[2,32,128]{2,1,0:T(8,128)S(1)} %constant_dynamic-update-slice_fusion.3), channel_id=1, source_target_pairs={{0,24},{8,0},{16,8},{24,16},{1,25},{9,1},{17,9},{25,17},{2,26},{10... | collective-permute-start | bytes 98312 | tf_op jit(solution)/shard_map/ppermute | solution.py:40
  70.9 1.6 %collective-permute-done.14 = f32[2,32,128]{2,1,0:T(8,128)S(1)} collective-permute-done((f32[2,32,128]{2,1,0:T(8,128)S(1)}, f32[2,32,128]{2,1,0:T(8,128)S(1)}, u32[]{:S(2)}, u32[]{:S(2)}) %collective-permute-start.14) | collective-permute-done | bytes 32800 | tf_op jit(solution)/shard_map/ppermute | solution.py:40
  72.5 3.5 %collective-permute-done.15 = f32[2,32,128]{2,1,0:T(8,128)S(1)} collective-permute-done((f32[2,32,128]{2,1,0:T(8,128)S(1)}, f32[2,32,128]{2,1,0:T(8,128)S(1)}, u32[]{:S(2)}, u32[]{:S(2)}) %collective-permute-start.15) | collective-permute-done | bytes 32800 | tf_op jit(solution)/shard_map/ppermute | solution.py:40
  76.1 1.2 collective-permute-done.16
  77.4 2.3 %collective-permute-start.17 = (f32[2,4,32,128]{3,2,1,0:T(8,128)S(1)}, f32[2,4,32,128]{3,2,1,0:T(8,128)S(1)}, u32[]{:S(2)}, u32[]{:S(2)}) collective-permute-start(f32[2,4,32,128]{3,2,1,0:T(8,128)S(1)} %pad_maximum_fusion.2.p0), channel_id=1, source_target_pairs={{0,64},{32,96},{64,128},{96,160},{128,192},{160,224},{192,0},{224,... | collective-permute-start | bytes 393224 | tf_op jit(solution)/shard_map/ppermute | solution.py:40
  79.7 2.2 %collective-permute-start.18 = (f32[2,4,32,128]{3,2,1,0:T(8,128)S(1)}, f32[2,4,32,128]{3,2,1,0:T(8,128)S(1)}, u32[]{:S(2)}, u32[]{:S(2)}) collective-permute-start(f32[2,4,32,128]{3,2,1,0:T(8,128)S(1)} %pad_maximum_fusion.2.p0), channel_id=1, source_target_pairs={{0,128},{32,160},{64,192},{96,224},{128,0},{160,32},{192,64},{224,... | collective-permute-start | bytes 393224 | tf_op jit(solution)/shard_map/ppermute | solution.py:40
  81.8 0.5 collective-permute-start.19
  82.4 1.8 %collective-permute-done.17.p1 = f32[2,4,32,128]{3,2,1,0:T(8,128)S(1)} collective-permute-done((f32[2,4,32,128]{3,2,1,0:T(8,128)S(1)}, f32[2,4,32,128]{3,2,1,0:T(8,128)S(1)}, u32[]{:S(2)}, u32[]{:S(2)}) %collective-permute-start.17) | collective-permute-done | bytes 131104 | tf_op jit(solution)/shard_map/ppermute | solution.py:40
  84.1 3.4 %collective-permute-done.18.p2 = f32[2,4,32,128]{3,2,1,0:T(8,128)S(1)} collective-permute-done((f32[2,4,32,128]{3,2,1,0:T(8,128)S(1)}, f32[2,4,32,128]{3,2,1,0:T(8,128)S(1)}, u32[]{:S(2)}, u32[]{:S(2)}) %collective-permute-start.18) | collective-permute-done | bytes 131104 | tf_op jit(solution)/shard_map/ppermute | solution.py:40
  87.6 1.7 %collective-permute-done.19.p3 = f32[2,4,32,128]{3,2,1,0:T(8,128)S(1)} collective-permute-done((f32[2,4,32,128]{3,2,1,0:T(8,128)S(1)}, f32[2,4,32,128]{3,2,1,0:T(8,128)S(1)}, u32[]{:S(2)}, u32[]{:S(2)}) %collective-permute-start.19) | collective-permute-done | bytes 131104 | tf_op jit(solution)/shard_map/ppermute | solution.py:40
  89.3 13.5 %shard_map.54 = (f32[4,16,128]{2,1,0:T(8,128)S(1)}, f32[2,2,8,128]{3,2,1,0:T(8,128)S(1)}) custom-call(f32[2,4,32,128]{3,2,1,0:T(8,128)S(1)} %pad_maximum_fusion.2.p0, f32[2,4,32,128]{3,2,1,0:T(8,128)S(1)} %collective-permute-done.17.p1, f32[2,4,32,128]{3,2,1,0:T(8,128)S(1)} %collective-permute-done.18.p2, f32[2,4,32,128]{3,2,1,0:T(8,128)S(1)} %collective-permute-done.19.p3), custom_call_target="tpu_custom_call" | custom-call | tf_op jit(solution)/shard_map/pallas_call | solution.py:72
  102.8 1.8 %collective-permute-start.20 = (f32[2,2,8,128]{3,2,1,0:T(8,128)S(1)}, f32[2,2,8,128]{3,2,1,0:T(8,128)S(1)}, u32[]{:S(2)}, u32[]{:S(2)}) collective-permute-start(f32[2,2,8,128]{3,2,1,0:T(8,128)S(1)} %get-tuple-element.33), channel_id=1, source_target_pairs={{0,1},{1,2},{2,3},{3,4},{4,5},{5,6},{6,7},{7,0},{8,9},{9,10},{10,1... | collective-permute-start | bytes 49160 | tf_op jit(solution)/shard_map/ppermute | solution.py:40
  104.6 2.3 %collective-permute-start.21 = (f32[2,2,8,128]{3,2,1,0:T(8,128)S(1)}, f32[2,2,8,128]{3,2,1,0:T(8,128)S(1)}, u32[]{:S(2)}, u32[]{:S(2)}) collective-permute-start(f32[2,2,8,128]{3,2,1,0:T(8,128)S(1)} %get-tuple-element.33), channel_id=1, source_target_pairs={{0,2},{1,3},{2,4},{3,5},{4,6},{5,7},{6,0},{7,1},{8,10},{9,11},{10,... | collective-permute-start | bytes 49160 | tf_op jit(solution)/shard_map/ppermute | solution.py:40
  106.9 0.5 collective-permute-start.22
  107.4 4.7 %collective-permute-start.23 = (f32[2,2,8,128]{3,2,1,0:T(8,128)S(1)}, f32[2,2,8,128]{3,2,1,0:T(8,128)S(1)}, u32[]{:S(2)}, u32[]{:S(2)}) collective-permute-start(f32[2,2,8,128]{3,2,1,0:T(8,128)S(1)} %get-tuple-element.33), channel_id=1, source_target_pairs={{0,4},{1,5},{2,6},{3,7},{4,0},{5,1},{6,2},{7,3},{8,12},{9,13},{10,... | collective-permute-start | bytes 49160 | tf_op jit(solution)/shard_map/ppermute | solution.py:40
  112.1 1.0 collective-permute-start.24
  113.2 2.4 %collective-permute-start.25 = (f32[2,2,8,128]{3,2,1,0:T(8,128)S(1)}, f32[2,2,8,128]{3,2,1,0:T(8,128)S(1)}, u32[]{:S(2)}, u32[]{:S(2)}) collective-permute-start(f32[2,2,8,128]{3,2,1,0:T(8,128)S(1)} %get-tuple-element.33), channel_id=1, source_target_pairs={{0,6},{1,7},{2,0},{3,1},{4,2},{5,3},{6,4},{7,5},{8,14},{9,15},{10,... | collective-permute-start | bytes 49160 | tf_op jit(solution)/shard_map/ppermute | solution.py:40
  115.5 1.7 %collective-permute-start.26 = (f32[2,2,8,128]{3,2,1,0:T(8,128)S(1)}, f32[2,2,8,128]{3,2,1,0:T(8,128)S(1)}, u32[]{:S(2)}, u32[]{:S(2)}) collective-permute-start(f32[2,2,8,128]{3,2,1,0:T(8,128)S(1)} %get-tuple-element.33), channel_id=1, source_target_pairs={{0,7},{1,0},{2,1},{3,2},{4,3},{5,4},{6,5},{7,6},{8,15},{9,8},{10,9... | collective-permute-start | bytes 49160 | tf_op jit(solution)/shard_map/ppermute | solution.py:40
  117.2 0.5 collective-permute-done.24
  118.1 1.2 collective-permute-done.26
  119.3 1.5 %collective-permute-start.28 = (f32[8,2,2,8,128]{4,3,2,1,0:T(8,128)S(1)}, f32[8,2,2,8,128]{4,3,2,1,0:T(8,128)S(1)}, u32[]{:S(2)}, u32[]{:S(2)}) collective-permute-start(f32[8,2,2,8,128]{4,3,2,1,0:T(8,128)S(1)} %constant_dynamic-update-slice_fusion.6.g0), channel_id=1, source_target_pairs={{0,16},{8,24},{16,0},{24,8},{1,17},{9,25},{17,1},{25,9},{2,18},{10... | collective-permute-start | bytes 393224 | tf_op jit(solution)/shard_map/ppermute | solution.py:40
  120.8 1.8 %collective-permute-start.29 = (f32[8,2,2,8,128]{4,3,2,1,0:T(8,128)S(1)}, f32[8,2,2,8,128]{4,3,2,1,0:T(8,128)S(1)}, u32[]{:S(2)}, u32[]{:S(2)}) collective-permute-start(f32[8,2,2,8,128]{4,3,2,1,0:T(8,128)S(1)} %constant_dynamic-update-slice_fusion.6.g0), channel_id=1, source_target_pairs={{0,24},{8,0},{16,8},{24,16},{1,25},{9,1},{17,9},{25,17},{2,26},{10... | collective-permute-start | bytes 393224 | tf_op jit(solution)/shard_map/ppermute | solution.py:40
  122.5 4.3 %collective-permute-done.27.g1 = f32[8,2,2,8,128]{4,3,2,1,0:T(8,128)S(1)} collective-permute-done((f32[8,2,2,8,128]{4,3,2,1,0:T(8,128)S(1)}, f32[8,2,2,8,128]{4,3,2,1,0:T(8,128)S(1)}, u32[]{:S(2)}, u32[]{:S(2)}) %collective-permute-start.27) | collective-permute-done | bytes 131104 | tf_op jit(solution)/shard_map/ppermute | solution.py:40
  126.9 0.9 collective-permute-done.29.g3
  127.8 7.6 %shard_map.55 = f32[4,16,32]{2,1,0:T(8,128)} custom-call(f32[8,2,2,8,128]{4,3,2,1,0:T(8,128)S(1)} %constant_dynamic-update-slice_fusion.6.g0, f32[8,2,2,8,128]{4,3,2,1,0:T(8,128)S(1)} %collective-permute-done.27.g1, f32[8,2,2,8,128]{4,3,2,1,0:T(8,128)S(1)} %collective-permute-done.28.g2, f32[8,2,2,8,128]{4,3,2,1,0:T(8,128)S(1)} %collective-permute-done.29.g3, ...), custom_call_target="tpu_custom_call" | custom-call | tf_op jit(solution)/shard_map/pallas_call | solution.py:72
  (49 shorter events, 1.6 us)
Async XLA Ops:
  0.6 8.3 %copy-start = (f32[16,64,128]{2,1,0:T(8,128)S(1)}, f32[16,64,128]{2,1,0:T(8,128)}, u32[]{:S(2)}) copy-start(f32[16,64,128]{2,1,0:T(8,128)} %rs.3) | copy-start | bytes 1572868
  0.6 8.3 %copy-start.1 = (f32[16,64,128]{2,1,0:T(8,128)S(1)}, f32[16,64,128]{2,1,0:T(8,128)}, u32[]{:S(2)}) copy-start(f32[16,64,128]{2,1,0:T(8,128)} %ab.3) | copy-start | bytes 1572868
  2.8 6.2 %collective-permute-start = (f32[9,64,128]{2,1,0:T(8,128)S(1)}, f32[9,64,128]{2,1,0:T(8,128)S(1)}, u32[]{:S(2)}, u32[]{:S(2)}) collective-permute-start(f32[9,64,128]{2,1,0:T(8,128)S(1)} %pad_maximum_fusion), channel_id=1, source_target_pairs={{0,32},{32,64},{64,96},{96,128},{128,160},{160,192},{192,224},{224... | collective-permute-start | bytes 884744 | tf_op jit(solution)/shard_map/ppermute | solution.py:40
  2.8 6.1 %collective-permute-start.1 = (f32[9,64,128]{2,1,0:T(8,128)S(1)}, f32[9,64,128]{2,1,0:T(8,128)S(1)}, u32[]{:S(2)}, u32[]{:S(2)}) collective-permute-start(f32[9,64,128]{2,1,0:T(8,128)S(1)} %pad_maximum_fusion.1), channel_id=1, source_target_pairs={{0,224},{32,0},{64,32},{96,64},{128,96},{160,128},{192,160},{224,1... | collective-permute-start | bytes 884744 | tf_op jit(solution)/shard_map/ppermute | solution.py:40
  9.0 9.1 %collective-permute-start.2 = (f32[230,128]{1,0:T(8,128)S(1)}, f32[230,128]{1,0:T(8,128)S(1)}, u32[]{:S(2)}, u32[]{:S(2)}) collective-permute-start(f32[230,128]{1,0:T(8,128)S(1)} %get-tuple-element.19), channel_id=1, source_target_pairs={{0,1},{1,2},{2,3},{3,4},{4,5},{5,6},{6,7},{7,0},{8,9},{9,10},{10,1... | collective-permute-start | bytes 353288 | tf_op jit(solution)/shard_map/ppermute | solution.py:40
  11.0 7.1 %collective-permute-start.3 = (f32[230,128]{1,0:T(8,128)S(1)}, f32[230,128]{1,0:T(8,128)S(1)}, u32[]{:S(2)}, u32[]{:S(2)}) collective-permute-start(f32[230,128]{1,0:T(8,128)S(1)} %get-tuple-element.20), channel_id=1, source_target_pairs={{0,7},{1,0},{2,1},{3,2},{4,3},{5,4},{6,5},{7,6},{8,15},{9,8},{10,9... | collective-permute-start | bytes 353288 | tf_op jit(solution)/shard_map/ppermute | solution.py:40
  19.2 6.5 %collective-permute-start.4 = (f32[2,80,128]{2,1,0:T(8,128)S(1)}, f32[2,80,128]{2,1,0:T(8,128)S(1)}, u32[]{:S(2)}, u32[]{:S(2)}) collective-permute-start(f32[2,80,128]{2,1,0:T(8,128)S(1)} %get-tuple-element.23), channel_id=1, source_target_pairs={{0,8},{8,16},{16,24},{24,0},{1,9},{9,17},{17,25},{25,1},{2,10},{10... | collective-permute-start | bytes 245768 | tf_op jit(solution)/shard_map/ppermute | solution.py:40
  20.9 4.8 %collective-permute-start.5 = (f32[2,80,128]{2,1,0:T(8,128)S(1)}, f32[2,80,128]{2,1,0:T(8,128)S(1)}, u32[]{:S(2)}, u32[]{:S(2)}) collective-permute-start(f32[2,80,128]{2,1,0:T(8,128)S(1)} %get-tuple-element.24), channel_id=1, source_target_pairs={{0,24},{8,0},{16,8},{24,16},{1,25},{9,1},{17,9},{25,17},{2,26},{10... | collective-permute-start | bytes 245768 | tf_op jit(solution)/shard_map/ppermute | solution.py:40
  39.0 3.9 %collective-permute-start.6 = (f32[5,32,128]{2,1,0:T(8,128)S(1)}, f32[5,32,128]{2,1,0:T(8,128)S(1)}, u32[]{:S(2)}, u32[]{:S(2)}) collective-permute-start(f32[5,32,128]{2,1,0:T(8,128)S(1)} %get-tuple-element.42), channel_id=1, source_target_pairs={{0,32},{32,64},{64,96},{96,128},{128,160},{160,192},{192,224},{224... | collective-permute-start | bytes 245768 | tf_op jit(solution)/shard_map/ppermute | solution.py:40
  39.0 3.9 %collective-permute-start.7 = (f32[5,32,128]{2,1,0:T(8,128)S(1)}, f32[5,32,128]{2,1,0:T(8,128)S(1)}, u32[]{:S(2)}, u32[]{:S(2)}) collective-permute-start(f32[5,32,128]{2,1,0:T(8,128)S(1)} %get-tuple-element.41), channel_id=1, source_target_pairs={{0,224},{32,0},{64,32},{96,64},{128,96},{160,128},{192,160},{224,1... | collective-permute-start | bytes 245768 | tf_op jit(solution)/shard_map/ppermute | solution.py:40
  42.9 5.7 %collective-permute-start.8 = (f32[18,8,128]{2,1,0:T(8,128)S(1)}, f32[18,8,128]{2,1,0:T(8,128)S(1)}, u32[]{:S(2)}, u32[]{:S(2)}) collective-permute-start(f32[18,8,128]{2,1,0:T(8,128)S(1)} %get-tuple-element.40), channel_id=1, source_target_pairs={{0,1},{1,2},{2,3},{3,4},{4,5},{5,6},{6,7},{7,0},{8,9},{9,10},{10,1... | collective-permute-start | bytes 221192 | tf_op jit(solution)/shard_map/ppermute | solution.py:40
  43.0 5.6 %collective-permute-start.9 = (f32[18,8,128]{2,1,0:T(8,128)S(1)}, f32[18,8,128]{2,1,0:T(8,128)S(1)}, u32[]{:S(2)}, u32[]{:S(2)}) collective-permute-start(f32[18,8,128]{2,1,0:T(8,128)S(1)} %get-tuple-element.39), channel_id=1, source_target_pairs={{0,7},{1,0},{2,1},{3,2},{4,3},{5,4},{6,5},{7,6},{8,15},{9,8},{10,9... | collective-permute-start | bytes 221192 | tf_op jit(solution)/shard_map/ppermute | solution.py:40
  49.1 5.8 %collective-permute-start.10 = (f32[2,48,128]{2,1,0:T(8,128)S(1)}, f32[2,48,128]{2,1,0:T(8,128)S(1)}, u32[]{:S(2)}, u32[]{:S(2)}) collective-permute-start(f32[2,48,128]{2,1,0:T(8,128)S(1)} %get-tuple-element.29), channel_id=1, source_target_pairs={{0,8},{8,16},{16,24},{24,0},{1,9},{9,17},{17,25},{25,1},{2,10},{10... | collective-permute-start | bytes 147464 | tf_op jit(solution)/shard_map/ppermute | solution.py:40
  50.8 4.2 %collective-permute-start.11 = (f32[2,48,128]{2,1,0:T(8,128)S(1)}, f32[2,48,128]{2,1,0:T(8,128)S(1)}, u32[]{:S(2)}, u32[]{:S(2)}) collective-permute-start(f32[2,48,128]{2,1,0:T(8,128)S(1)} %get-tuple-element.30), channel_id=1, source_target_pairs={{0,24},{8,0},{16,8},{24,16},{1,25},{9,1},{17,9},{25,17},{2,26},{10... | collective-permute-start | bytes 147464 | tf_op jit(solution)/shard_map/ppermute | solution.py:40
  61.2 4.9 %collective-permute-start.12 = (f32[2,8,128]{2,1,0:T(8,128)S(1)}, f32[2,8,128]{2,1,0:T(8,128)S(1)}, u32[]{:S(2)}, u32[]{:S(2)}) collective-permute-start(f32[2,8,128]{2,1,0:T(8,128)S(1)} %get-tuple-element.46), channel_id=1, source_target_pairs={{0,1},{1,2},{2,3},{3,4},{4,5},{5,6},{6,7},{7,0},{8,9},{9,10},{10,1... | collective-permute-start | bytes 24584 | tf_op jit(solution)/shard_map/ppermute | solution.py:40
  64.2 3.8 %collective-permute-start.13 = (f32[2,8,128]{2,1,0:T(8,128)S(1)}, f32[2,8,128]{2,1,0:T(8,128)S(1)}, u32[]{:S(2)}, u32[]{:S(2)}) collective-permute-start(f32[2,8,128]{2,1,0:T(8,128)S(1)} %get-tuple-element.45), channel_id=1, source_target_pairs={{0,7},{1,0},{2,1},{3,2},{4,3},{5,4},{6,5},{7,6},{8,15},{9,8},{10,9... | collective-permute-start | bytes 24584 | tf_op jit(solution)/shard_map/ppermute | solution.py:40
  68.0 4.5 %collective-permute-start.14 = (f32[2,32,128]{2,1,0:T(8,128)S(1)}, f32[2,32,128]{2,1,0:T(8,128)S(1)}, u32[]{:S(2)}, u32[]{:S(2)}) collective-permute-start(f32[2,32,128]{2,1,0:T(8,128)S(1)} %constant_dynamic-update-slice_fusion.3), channel_id=1, source_target_pairs={{0,24},{8,0},{16,8},{24,16},{1,25},{9,1},{17,9},{25,17},{2,26},{10... | collective-permute-start | bytes 98312 | tf_op jit(solution)/shard_map/ppermute | solution.py:40
  70.9 5.1 %collective-permute-start.15 = (f32[2,32,128]{2,1,0:T(8,128)S(1)}, f32[2,32,128]{2,1,0:T(8,128)S(1)}, u32[]{:S(2)}, u32[]{:S(2)}) collective-permute-start(f32[2,32,128]{2,1,0:T(8,128)S(1)} %constant_dynamic-update-slice_fusion.3), channel_id=1, source_target_pairs={{0,8},{8,16},{16,24},{24,0},{1,9},{9,17},{17,25},{25,1},{2,10},{10... | collective-permute-start | bytes 98312 | tf_op jit(solution)/shard_map/ppermute | solution.py:40
  76.0 1.3 collective-permute-start.16
  77.4 6.8 %collective-permute-start.17 = (f32[2,4,32,128]{3,2,1,0:T(8,128)S(1)}, f32[2,4,32,128]{3,2,1,0:T(8,128)S(1)}, u32[]{:S(2)}, u32[]{:S(2)}) collective-permute-start(f32[2,4,32,128]{3,2,1,0:T(8,128)S(1)} %pad_maximum_fusion.2.p0), channel_id=1, source_target_pairs={{0,64},{32,96},{64,128},{96,160},{128,192},{160,224},{192,0},{224,... | collective-permute-start | bytes 393224 | tf_op jit(solution)/shard_map/ppermute | solution.py:40
  79.7 7.9 %collective-permute-start.18 = (f32[2,4,32,128]{3,2,1,0:T(8,128)S(1)}, f32[2,4,32,128]{3,2,1,0:T(8,128)S(1)}, u32[]{:S(2)}, u32[]{:S(2)}) collective-permute-start(f32[2,4,32,128]{3,2,1,0:T(8,128)S(1)} %pad_maximum_fusion.2.p0), channel_id=1, source_target_pairs={{0,128},{32,160},{64,192},{96,224},{128,0},{160,32},{192,64},{224,... | collective-permute-start | bytes 393224 | tf_op jit(solution)/shard_map/ppermute | solution.py:40
  81.8 7.4 %collective-permute-start.19 = (f32[2,4,32,128]{3,2,1,0:T(8,128)S(1)}, f32[2,4,32,128]{3,2,1,0:T(8,128)S(1)}, u32[]{:S(2)}, u32[]{:S(2)}) collective-permute-start(f32[2,4,32,128]{3,2,1,0:T(8,128)S(1)} %pad_maximum_fusion.2.p0), channel_id=1, source_target_pairs={{0,192},{32,224},{64,0},{96,32},{128,64},{160,96},{192,128},{224,1... | collective-permute-start | bytes 393224 | tf_op jit(solution)/shard_map/ppermute | solution.py:40
  102.8 10.4 %collective-permute-start.20 = (f32[2,2,8,128]{3,2,1,0:T(8,128)S(1)}, f32[2,2,8,128]{3,2,1,0:T(8,128)S(1)}, u32[]{:S(2)}, u32[]{:S(2)}) collective-permute-start(f32[2,2,8,128]{3,2,1,0:T(8,128)S(1)} %get-tuple-element.33), channel_id=1, source_target_pairs={{0,1},{1,2},{2,3},{3,4},{4,5},{5,6},{6,7},{7,0},{8,9},{9,10},{10,1... | collective-permute-start | bytes 49160 | tf_op jit(solution)/shard_map/ppermute | solution.py:40
  104.6 10.9 %collective-permute-start.21 = (f32[2,2,8,128]{3,2,1,0:T(8,128)S(1)}, f32[2,2,8,128]{3,2,1,0:T(8,128)S(1)}, u32[]{:S(2)}, u32[]{:S(2)}) collective-permute-start(f32[2,2,8,128]{3,2,1,0:T(8,128)S(1)} %get-tuple-element.33), channel_id=1, source_target_pairs={{0,2},{1,3},{2,4},{3,5},{4,6},{5,7},{6,0},{7,1},{8,10},{9,11},{10,... | collective-permute-start | bytes 49160 | tf_op jit(solution)/shard_map/ppermute | solution.py:40
  106.9 10.3 %collective-permute-start.22 = (f32[2,2,8,128]{3,2,1,0:T(8,128)S(1)}, f32[2,2,8,128]{3,2,1,0:T(8,128)S(1)}, u32[]{:S(2)}, u32[]{:S(2)}) collective-permute-start(f32[2,2,8,128]{3,2,1,0:T(8,128)S(1)} %get-tuple-element.33), channel_id=1, source_target_pairs={{0,3},{1,4},{2,5},{3,6},{4,7},{5,0},{6,1},{7,2},{8,11},{9,12},{10,... | collective-permute-start | bytes 49160 | tf_op jit(solution)/shard_map/ppermute | solution.py:40
  107.4 9.8 %collective-permute-start.23 = (f32[2,2,8,128]{3,2,1,0:T(8,128)S(1)}, f32[2,2,8,128]{3,2,1,0:T(8,128)S(1)}, u32[]{:S(2)}, u32[]{:S(2)}) collective-permute-start(f32[2,2,8,128]{3,2,1,0:T(8,128)S(1)} %get-tuple-element.33), channel_id=1, source_target_pairs={{0,4},{1,5},{2,6},{3,7},{4,0},{5,1},{6,2},{7,3},{8,12},{9,13},{10,... | collective-permute-start | bytes 49160 | tf_op jit(solution)/shard_map/ppermute | solution.py:40
  112.1 5.6 %collective-permute-start.24 = (f32[2,2,8,128]{3,2,1,0:T(8,128)S(1)}, f32[2,2,8,128]{3,2,1,0:T(8,128)S(1)}, u32[]{:S(2)}, u32[]{:S(2)}) collective-permute-start(f32[2,2,8,128]{3,2,1,0:T(8,128)S(1)} %get-tuple-element.33), channel_id=1, source_target_pairs={{0,5},{1,6},{2,7},{3,0},{4,1},{5,2},{6,3},{7,4},{8,13},{9,14},{10,... | collective-permute-start | bytes 49160 | tf_op jit(solution)/shard_map/ppermute | solution.py:40
  113.2 4.9 %collective-permute-start.25 = (f32[2,2,8,128]{3,2,1,0:T(8,128)S(1)}, f32[2,2,8,128]{3,2,1,0:T(8,128)S(1)}, u32[]{:S(2)}, u32[]{:S(2)}) collective-permute-start(f32[2,2,8,128]{3,2,1,0:T(8,128)S(1)} %get-tuple-element.33), channel_id=1, source_target_pairs={{0,6},{1,7},{2,0},{3,1},{4,2},{5,3},{6,4},{7,5},{8,14},{9,15},{10,... | collective-permute-start | bytes 49160 | tf_op jit(solution)/shard_map/ppermute | solution.py:40
  115.5 3.7 %collective-permute-start.26 = (f32[2,2,8,128]{3,2,1,0:T(8,128)S(1)}, f32[2,2,8,128]{3,2,1,0:T(8,128)S(1)}, u32[]{:S(2)}, u32[]{:S(2)}) collective-permute-start(f32[2,2,8,128]{3,2,1,0:T(8,128)S(1)} %get-tuple-element.33), channel_id=1, source_target_pairs={{0,7},{1,0},{2,1},{3,2},{4,3},{5,4},{6,5},{7,6},{8,15},{9,8},{10,9... | collective-permute-start | bytes 49160 | tf_op jit(solution)/shard_map/ppermute | solution.py:40
  119.3 7.6 %collective-permute-start.27 = (f32[8,2,2,8,128]{4,3,2,1,0:T(8,128)S(1)}, f32[8,2,2,8,128]{4,3,2,1,0:T(8,128)S(1)}, u32[]{:S(2)}, u32[]{:S(2)}) collective-permute-start(f32[8,2,2,8,128]{4,3,2,1,0:T(8,128)S(1)} %constant_dynamic-update-slice_fusion.6.g0), channel_id=1, source_target_pairs={{0,8},{8,16},{16,24},{24,0},{1,9},{9,17},{17,25},{25,1},{2,10},{10... | collective-permute-start | bytes 393224 | tf_op jit(solution)/shard_map/ppermute | solution.py:40
  119.3 7.6 %collective-permute-start.28 = (f32[8,2,2,8,128]{4,3,2,1,0:T(8,128)S(1)}, f32[8,2,2,8,128]{4,3,2,1,0:T(8,128)S(1)}, u32[]{:S(2)}, u32[]{:S(2)}) collective-permute-start(f32[8,2,2,8,128]{4,3,2,1,0:T(8,128)S(1)} %constant_dynamic-update-slice_fusion.6.g0), channel_id=1, source_target_pairs={{0,16},{8,24},{16,0},{24,8},{1,17},{9,25},{17,1},{25,9},{2,18},{10... | collective-permute-start | bytes 393224 | tf_op jit(solution)/shard_map/ppermute | solution.py:40
  120.8 7.0 %collective-permute-start.29 = (f32[8,2,2,8,128]{4,3,2,1,0:T(8,128)S(1)}, f32[8,2,2,8,128]{4,3,2,1,0:T(8,128)S(1)}, u32[]{:S(2)}, u32[]{:S(2)}) collective-permute-start(f32[8,2,2,8,128]{4,3,2,1,0:T(8,128)S(1)} %constant_dynamic-update-slice_fusion.6.g0), channel_id=1, source_target_pairs={{0,24},{8,0},{16,8},{24,16},{1,25},{9,1},{17,9},{25,17},{2,26},{10... | collective-permute-start | bytes 393224 | tf_op jit(solution)/shard_map/ppermute | solution.py:40

commit v2 on v0

v2 whole, which is shorter than its diff:
```python
import jax
import jax.numpy as jnp
from jax import lax
from jax.experimental import pallas as pl
from jax.experimental.pallas import tpu as pltpu
from jax.sharding import PartitionSpec as P

DEGREE = 4
LEVELS = 3
BOTTOM_ITERS = 20

smooth_low = 1.5
smooth_top = 12.0
absorb_top = 1.0
bottom_low = 0.008

F32 = jnp.float32
HALO = 5
WIDE = 15
LANES = 128


def cheb_tables(count, lower, upper):
    theta = (upper + lower) / 2.0
    delta = (upper - lower) / 2.0
    sigma = theta / delta
    rho_value = 1.0 / sigma
    firsts = []
    seconds = []
    for turn_index in range(count - 1):
        rho_next = 1.0 / (2.0 * sigma - rho_value)
        firsts.append(rho_next * rho_value)
        seconds.append(2.0 * rho_next / delta)
        rho_value = rho_next
    return (1.0 / theta, firsts, seconds)


def shift(value, axis, step):
    count = lax.axis_size(axis)
    return lax.ppermute(value, axis, [(i, (i + step) % count) for i in range(count)])


def flag(condition):
    return jnp.where(condition, 1.0, 0.0).astype(F32)


def edges(axis):
    index = lax.axis_index(axis)
    return flag(index > 0), flag(index < lax.axis_size(axis) - 1)


def lane_iota(rows):
    return lax.broadcasted_iota(jnp.int32, (rows, LANES), 1)


def row_iota(rows):
    return lax.broadcasted_iota(jnp.int32, (rows, LANES), 0)


def pair_sum(out_start, count):
    row = lax.broadcasted_iota(jnp.int32, (LANES, LANES), 0)
    column = lax.broadcasted_iota(jnp.int32, (LANES, LANES), 1) - out_start
    hit = (row // 2 == column) & (column >= 0) & (column < count)
    return jnp.where(hit, 0.5, 0.0).astype(F32)


def exact_dot(a, b):
    return jnp.dot(a, b, preferred_element_type=F32, precision=lax.Precision.HIGHEST)


def call(kernel, outs, scratch, *args):
    result = pl.pallas_call(
        kernel,
        out_shape=[jax.ShapeDtypeStruct(s, F32) for s in outs],
        in_specs=[pl.BlockSpec(memory_space=pltpu.VMEM)] * len(args),
        out_specs=[pl.BlockSpec(memory_space=pltpu.VMEM)] * len(outs),
        scratch_shapes=[pltpu.VMEM(s, F32) for s in scratch],
        compiler_params=pltpu.CompilerParams(vmem_limit_bytes=32 << 20),
    )(*args)
    return result


def step_tables(level_top, count=DEGREE + 1, low=smooth_low):
    start_scale, firsts, seconds = cheb_tables(count, low, level_top)
    tables = []
    for k, (a, b) in enumerate(zip(firsts, seconds)):
        if k == 0:
            scale = b * start_scale
            tables.append((scale, ((1.0 + a) * start_scale + b) / scale, 0.0, 0.0))
        elif k == 1:
            tables.append((b, (1.0 + a) / b, (b - a * start_scale) / b, 0.0))
        else:
            tables.append((b, (1.0 + a) / b, 1.0, a))
    return tables


def combine(table, around, value, coef, source, old, scale):
    _, pull, lift, back = table
    inner = around - (coef - pull) * value
    if lift == 1.0:
        inner = inner + source()
    elif lift:
        inner = inner + lift * source()
    out = scale * inner
    if back:
        out = out - back * old()
    return out


def clear_pads(ref, planes, first, last):
    for p in range(planes):
        ref[p, 0:first, :] = jnp.zeros((first, LANES), F32)
        ref[p, last : last + 8, :] = jnp.zeros((8, LANES), F32)


def rolled(value, amount):
    amount = amount % LANES
    return pltpu.roll(value, amount, 1) if amount else value


def fold_rows(tmp, rows):
    return tmp[pl.ds(0, rows, stride=2), :] + tmp[pl.ds(1, rows, stride=2), :]


S0_PLANES = list(range(1, 25))
C0_PLANES = list(range(2, 24))
STRIPS0 = [("s", p) for p in S0_PLANES] + [("c", p) for p in C0_PLANES]


def strip_at(name, p):
    return 128 + 5 * STRIPS0.index((name, p))


def before_kernel(rs, ab, low, high, c1, tmp, gathered):
    lane = lane_iota(32)
    for i in range(8):
        tmp[...] = ab[2 * i, :, :] + ab[2 * i + 1, :, :]
        gathered[32 * i : 32 * i + 32, :] = fold_rows(tmp, 32)
    low[0:5, :, :] = rs[0:5, :, :]
    low[5:9, :, :] = ab[0:4, :, :]
    high[0:5, :, :] = rs[11:16, :, :]
    high[5:9, :, :] = ab[12:16, :, :]
    folded = exact_dot(gathered[...], pair_sum(0, 64))
    for j in range(4):
        first = folded[64 * j : 64 * j + 32, :]
        second = folded[64 * j + 32 : 64 * j + 64, :]
        pair = jnp.where(lane < 64, first, pltpu.roll(second, 64, 1))
        c1[j, :, :] = pair
        target = low if j < 2 else high
        target[9, 32 * (j % 2) : 32 * (j % 2) + 32, :] = pair


def plane0(name, p, rs, ab, fl, fr):
    if name == "s":
        if p < 5:
            return fl, p
        if p < 21:
            return rs, p - 5
        return fr, p - 21
    if p < 5:
        return fl, 5 + p - 1
    if p < 21:
        return ab, p - 5
    return fr, 5 + p - 21


def c1_pair(j, c1, fl, fr):
    if j < 2:
        return fl[9, 32 * j : 32 * j + 32, :]
    if j < 6:
        return c1[j - 2, :, :]
    return fr[9, 32 * (j - 6) : 32 * (j - 6) + 32, :]


def z_strips_kernel(rs, ab, c1, fl, fr, low, high):
    for j in range(8):
        pair = c1_pair(j, c1, fl, fr)
        low[16 * j : 16 * j + 16, :] = pair[0:16, :]
        high[16 * j : 16 * j + 16, :] = pair[16:32, :]
    for name, p in STRIPS0:
        ref, q = plane0(name, p, rs, ab, fl, fr)
        at = strip_at(name, p)
        low[at : at + 5, :] = ref[q, 0:5, :]
        high[at : at + 5, :] = ref[q, 59:64, :]


def wide_place(p):
    if 5 <= p < 13:
        return 0, WIDE * (p - 5), WIDE
    outer = [q for q in range(18) if q < 5 or q > 12]
    widths = [WIDE - (5 - q if q < 5 else q - 12) for q in outer]
    n = outer.index(p)
    return 1, sum(widths[:n]), widths[n]


def wide_pair(p):
    if p in (0, 17):
        return 8, p // 17
    return (p - 1) // 2, (p - 1) % 2


def pack_wide(pairs, planes, low, high, at):
    lane = lane_iota(64)
    for t in range(2):
        low_tile = jnp.zeros((64, LANES), F32)
        high_tile = jnp.zeros((64, LANES), F32)
        for p in planes:
            tile, start, width = wide_place(p)
            if tile != t:
                continue
            pair, half = wide_pair(p)
            value = pairs[pair, :, :]
            inside = (lane >= start) & (lane < start + width)
            low_tile = jnp.where(inside, rolled(value, start - 64 * half), low_tile)
            high_tile = jnp.where(
                inside, rolled(value, start - 64 * half - (64 - width)), high_tile
            )
        low[at + 64 * t : at + 64 * t + 64, :] = low_tile
        high[at + 64 * t : at + 64 * t + 64, :] = high_tile


def build0_kernel(rs, ab, c1, fl, fr, zl, zh, es, ec, low, high, c1e):
    x_low, x_high = edges("gx")
    z_low, z_high = edges("gz")
    zero = jnp.zeros((16, LANES), F32)
    for p in range(26):
        ref, q = plane0("s", p, rs, ab, fl, fr)
        scale = x_low if p < 5 else (x_high if p > 20 else None)
        value = ref[q, :, :]
        es[p, 16:80, :] = value if scale is None else value * scale
        es[p, 0:16, :] = zero
        es[p, 80:96, :] = zero
        if p in S0_PLANES:
            at = strip_at("s", p)
            below, above = zl[at : at + 5, :] * z_low, zh[at : at + 5, :] * z_high
            if scale is not None:
                below, above = below * scale, above * scale
            es[p, 11:16, :] = below
            es[p, 80:85, :] = above
    for p in range(1, 25):
        ref, q = plane0("c", p, rs, ab, fl, fr)
        ec[p, 16:80, :] = ref[q, :, :] + 6.0
        ec[p, 0:16, :] = zero
        ec[p, 80:96, :] = zero
        if p in C0_PLANES:
            at = strip_at("c", p)
            ec[p, 11:16, :] = zl[at : at + 5, :] + 6.0
            ec[p, 80:85, :] = zh[at : at + 5, :] + 6.0
    lane = lane_iota(16)
    for t, ref in enumerate((es, ec)):
        for r in range(0, 80, 16):
            low_tile = jnp.zeros((16, LANES), F32)
            high_tile = jnp.zeros((16, LANES), F32)
            for p in S0_PLANES:
                value = pltpu.roll(ref[p, 8 + r : 24 + r, :], 5 * p, 1)
                low_tile = jnp.where((lane >= 5 * p) & (lane < 5 * p + 5), value, low_tile)
                high_tile = jnp.where((lane >= 5 * p - 5) & (lane < 5 * p), value, high_tile)
            low[80 * t + r : 80 * t + r + 16, :] = low_tile
            high[80 * t + r : 80 * t + r + 16, :] = high_tile
    for j in range(8):
        c1e[j, 0:16, :] = zl[16 * j : 16 * j + 16, :]
        c1e[j, 16:48, :] = c1_pair(j, c1, fl, fr)
        c1e[j, 48:64, :] = zh[16 * j : 16 * j + 16, :]
    pack_wide(c1e, range(1, 17), low, high, 160)


def level0_kernel(
    es, ec, low_sent, high_sent, yl, yh, it0, s1, low, high,
    a0, b0, sl, sr, al, ar, bl, br, cl, cr, hz, tmp, gathered,
):
    x_low, x_high = edges("gx")
    y_low, y_high = edges("gy")
    z_low, z_high = edges("gz")
    lane = lane_iota(16)
    fifth = (lane * 52429) >> 18
    in_five = lane - 5 * fifth
    row = row_iota(16)
    first_rows = jnp.where(row < 8, z_low, 1.0)
    last_rows = jnp.where(row >= 8, z_high, 1.0)
    chunks = list(range(0, 80, 16))

    def row_mask(r):
        return first_rows if r == 0 else (last_rows if r == 64 else None)

    def plane_mask(p):
        return jnp.where(p < 5, x_low, jnp.where(p > 20, x_high, 1.0))

    left_ok = jnp.where(lane < 120, plane_mask(fifth + 1), 0.0) * y_low
    right_ok = jnp.where((lane >= 5) & (lane < 125), plane_mask(fifth), 0.0) * y_high

    def side_mask(r):
        rows_ok = row_mask(r)
        if rows_ok is None:
            return left_ok, right_ok
        return left_ok * rows_ok, right_ok * rows_ok

    for ref in (sl, sr, al, ar, bl, br):
        ref[0:8, :] = jnp.zeros((8, LANES), F32)
        ref[88:96, :] = jnp.zeros((8, LANES), F32)
    strips = []
    for r in chunks:
        left_mask, right_mask = side_mask(r)
        sl[8 + r : 24 + r, :] = yl[r : r + 16, :] * left_mask
        sr[8 + r : 24 + r, :] = yh[r : r + 16, :] * right_mask
        cl[r : r + 16, :] = yl[80 + r : 96 + r, :]
        cr[r : r + 16, :] = yh[80 + r : 96 + r, :]
        strips.append(
            jnp.where(in_five == 4, high_sent[r : r + 16, :], low_sent[r : r + 16, :])
        )
    clear_pads(a0, 26, 8, 88)
    clear_pads(b0, 26, 8, 88)

    def mix(left, right):
        for r in chunks:
            hz[r : r + 16, :] = jnp.where(
                in_five == 4,
                pltpu.roll(right[8 + r : 24 + r, :], LANES - 1, 1),
                pltpu.roll(left[8 + r : 24 + r, :], 1, 1),
            )

    def around_own(now, p, r, rows=16):
        here = 8 + r
        value = now[p, here : here + rows, :]
        beyond = pltpu.roll(hz[r : r + rows, :], LANES - 5 * p, 1)
        right = jnp.where(lane == LANES - 1, beyond, pltpu.roll(value, LANES - 1, 1))
        left = jnp.where(lane == 0, beyond, pltpu.roll(value, 1, 1))
        total = (
            (right + left)
            + (now[p - 1, here : here + rows, :] + now[p + 1, here : here + rows, :])
            + (now[p, here - 1 : here - 1 + rows, :] + now[p, here + 1 : here + 1 + rows, :])
        )
        return total, value

    tables = step_tables(smooth_top + absorb_top)
    now, left_now, right_now = es, sl, sr
    for k, table in enumerate(tables):
        target, left_to, right_to = ((a0, al, ar), (b0, bl, br))[k % 2]
        mix(left_now, right_now)
        for r, strip in zip(chunks, strips):
            here = 8 + r
            for side, mask, ref, to, source, coef in zip(
                range(2), side_mask(r), (left_now, right_now), (left_to, right_to), (sl, sr), (cl, cr)
            ):
                value = ref[here : here + 16, :]
                if side == 0:
                    right = pltpu.roll(jnp.where(in_five == 0, strip, value), LANES - 1, 1)
                    left = pltpu.roll(value, 1, 1)
                else:
                    right = pltpu.roll(value, LANES - 1, 1)
                    left = pltpu.roll(jnp.where(in_five == 4, strip, value), 1, 1)
                total = (
                    (right + left)
                    + (pltpu.roll(value, 5, 1) + pltpu.roll(value, LANES - 5, 1))
                    + (ref[here - 1 : here + 15, :] + ref[here + 1 : here + 17, :])
                )
                to[here : here + 16, :] = combine(
                    table, total, value, coef[r : r + 16, :],
                    lambda: source[here : here + 16, :],
                    lambda: to[here : here + 16, :],
                    mask * table[0],
                )

        trips = 3 if k == 0 else 2
        each = (24 - 2 * k) // trips

        def body(i, carry, now=now, target=target, table=table, k=k, each=each):
            carry = list(carry)
            for q in range(each):
                p = k + 1 + each * i + q
                scale = table[0] * plane_mask(p)
                for r in chunks:
                    total, value = around_own(now, p, r)
                    here = 8 + r
                    rows_ok = row_mask(r)
                    new = combine(
                        table, total, value, ec[p, here : here + 16, :],
                        lambda: es[p, here : here + 16, :],
                        lambda: target[p, here : here + 16, :],
                        scale if rows_ok is None else scale * rows_ok,
                    )
                    target[p, here : here + 16, :] = new
            for q in range(each if k < DEGREE - 1 else 0):
                p = k + 1 + each * i + q
                kept = (lane == 5 * p) | (lane == 5 * p - 1)
                for n, r in enumerate(chunks):
                    edge = pltpu.roll(target[p, 8 + r : 24 + r, :], 5 * p, 1)
                    carry[n] = jnp.where(kept, edge, carry[n])
            return tuple(carry)

        empty = tuple(jnp.zeros((16, LANES), F32) for _ in chunks)
        strips = lax.fori_loop(0, trips, body, empty)
        now, left_now, right_now = target, left_to, right_to
    mix(left_now, right_now)

    def finish(i, carry):
        for r in range(8, 72, 16):
            total = None
            for half in range(2):
                p = 5 + 2 * i + half
                around, value = around_own(now, p, r)
                it0[2 * i + half, r - 8 : r + 8, :] = value
                here = 8 + r
                left_over = (
                    es[p, here : here + 16, :] - ec[p, here : here + 16, :] * value + around
                )
                total = left_over if total is None else total + left_over
            tmp[r - 8 : r + 8, :] = total
        gathered[pl.ds(pl.multiple_of(32 * i, 32), 32), :] = fold_rows(tmp, 32)
        return carry

    lax.fori_loop(0, 8, finish, 0)
    folded = exact_dot(gathered[...], pair_sum(0, 64))
    lane32 = lane_iota(32)
    for j in range(4):
        first = folded[64 * j : 64 * j + 32, :]
        second = folded[64 * j + 32 : 64 * j + 64, :]
        pair = jnp.where(lane32 < 64, first, pltpu.roll(second, 64, 1))
        s1[j, :, :] = pair
        if j < 3:
            low[j, :, :] = pair
        if j > 0:
            high[j - 1, :, :] = pair


def s1_pair(j, s1, fl, fr):
    if j < 2:
        return fl[1 + j, :, :]
    if j < 6:
        return s1[j - 2, :, :]
    if j < 8:
        return fr[j - 6, :, :]
    return jnp.where(
        lane_iota(32) < 64, pltpu.roll(fl[0, :, :], 64, 1), pltpu.roll(fr[2, :, :], 64, 1)
    )


def z_strips1_kernel(s1, fl, fr, low, high):
    for j in range(9):
        pair = s1_pair(j, s1, fl, fr)
        low[16 * j : 16 * j + 16, :] = pair[0:16, :]
        high[16 * j : 16 * j + 16, :] = pair[16:32, :]


def build1_kernel(s1, fl, fr, zl, zh, ext, low, high):
    for j in range(9):
        ext[j, 0:16, :] = zl[16 * j : 16 * j + 16, :]
        ext[j, 16:48, :] = s1_pair(j, s1, fl, fr)
        ext[j, 48:64, :] = zh[16 * j : 16 * j + 16, :]
    pack_wide(ext, range(18), low, high, 0)


def level1_kernel(
    ext, yl, yh, c1e, low0, high0, it1, piece, es, ec, a, b, tmp, gathered
):
    x_low, x_high = edges("gx")
    y_low, y_high = edges("gy")
    z_low, z_high = edges("gz")
    lane = lane_iota(64)
    row = row_iota(64)
    ok_rows = jnp.where(row < 16, z_low, jnp.where(row >= 48, z_high, 1.0))
    ok_lanes = jnp.where(lane < 64, 1.0, jnp.where(lane < 96, y_high, y_low))
    ok = ok_rows * ok_lanes
    for p in range(18):
        t, at_lane, width = wide_place(p)
        pair, half = wide_pair(p)
        for kind, (pairs, below, above, base) in enumerate(
            ((ext, yl, yh, 0), (c1e, low0, high0, 160))
        ):
            if kind == 1 and p in (0, 17):
                continue
            mine = rolled(pairs[pair, :, :], 64 * half)
            at = base + 64 * t
            from_low = rolled(below[at : at + 64, :], LANES - width - at_lane)
            from_high = rolled(above[at : at + 64, :], 64 - at_lane)
            full = jnp.where(
                lane < 64,
                mine,
                jnp.where(
                    lane < 64 + width,
                    from_high,
                    jnp.where(lane >= LANES - width, from_low, 0.0),
                ),
            )
            if kind == 0:
                full = full * ok
                if p < 5:
                    full = full * x_low
                if p > 12:
                    full = full * x_high
                es[p, 8:72, :] = full
            else:
                ec[p, 8:72, :] = full + 6.0
                if 5 <= p < 13:
                    if p % 2 == 1:
                        tmp[...] = full
                    else:
                        tmp[...] = tmp[...] + full
                        j = (p - 5) // 2
                        gathered[128 + 32 * j : 160 + 32 * j, :] = fold_rows(tmp, 32)
    lane32 = lane_iota(32)
    clear_pads(es, 18, 8, 72)
    clear_pads(a, 18, 8, 72)
    clear_pads(b, 18, 8, 72)

    def around_of(now, p, start, rows):
        here = slice(start, start + rows)
        value = now[p, here, :]
        total = (
            (pltpu.roll(value, LANES - 1, 1) + pltpu.roll(value, 1, 1))
            + (now[p - 1, here, :] + now[p + 1, here, :])
            + (now[p, start - 1 : start - 1 + rows, :] + now[p, start + 1 : start + 1 + rows, :])
        )
        return total, value

    now = es
    for k, table in enumerate(step_tables(smooth_top + 4.0 * absorb_top)):
        target = (a, b)[k % 2]

        trips = 4 if k == 0 else 2
        each = (16 - 2 * k) // trips

        def body(i, carry, now=now, target=target, table=table, k=k, each=each):
            for q in range(each):
                p = k + 1 + each * i + q
                scale = table[0] * jnp.where(p < 5, x_low, jnp.where(p > 12, x_high, 1.0))
                for start in range(8, 72, 16):
                    here = slice(start, start + 16)
                    total, value = around_of(now, p, start, 16)
                    target[p, here, :] = combine(
                        table, total, value, ec[p, here, :],
                        lambda: es[p, here, :],
                        lambda: target[p, here, :],
                        ok[start - 8 : start + 8, :] * scale,
                    )
            return carry

        lax.fori_loop(0, trips, body, 0)
        now = target
    for i in range(4):
        for start in range(8, 72, 16):
            total = None
            for half in range(2):
                p = 5 + 2 * i + half
                around, value = around_of(now, p, start, 16)
                here = slice(start, start + 16)
                left_over = es[p, here, :] - ec[p, here, :] * value + around
                total = left_over if total is None else total + left_over
                if 24 <= start < 56:
                    it1[2 * i + half, start - 24 : start - 8, :] = value[:, 0:64]
            tmp[start - 8 : start + 8, :] = total
        gathered[32 * i : 32 * i + 32, :] = fold_rows(tmp, 32)
    j = lax.broadcasted_iota(jnp.int32, (LANES, LANES), 0)
    column = lax.broadcasted_iota(jnp.int32, (LANES, LANES), 1)
    goes_to = jnp.where(j < 74, j // 2 + 5, jnp.where(j >= 118, (j - 118) // 2, -1))
    folded = exact_dot(gathered[...], jnp.where(goes_to == column, 0.5, 0.0).astype(F32))
    for kind in range(2):
        for half in range(2):
            at = 128 * kind + 64 * half
            first, second = folded[at : at + 32, :], folded[at + 32 : at + 64, :]
            piece[2 * kind + half, :, :] = jnp.where(lane32 < 64, first, pltpu.roll(second, 64, 1))


def level2_kernel(mine, other, it2, piece, es, ec, a, b, tmp, gathered):
    gx = lax.axis_index("gx")
    y_low, y_high = edges("gy")
    z_low, z_high = edges("gz")
    chip, core = gx // 2, gx % 2
    lane = lane_iota(32)
    row = row_iota(32)
    place = lane % 64
    ok_rows = jnp.where(row < 8, z_low, jnp.where(row >= 24, z_high, 1.0))
    ok_lanes = jnp.where(
        place < 5, y_low, jnp.where(place < 37, 1.0, jnp.where(place < 42, y_high, 0.0))
    )
    ok = ok_rows * ok_lanes
    for ref in (es, a, b):
        for p in (0, 17):
            ref[p, :, :] = jnp.zeros((48, LANES), F32)
        clear_pads(ref, 18, 8, 40)
    for j, pieces in enumerate((mine, other)):
        for k in range(4):
            owner = 2 * ((chip - k + 4) % 4) + (core + j) % 2
            for t in range(2):
                tile = 2 * owner + t
                es[1 + tile, 8:40, :] = pieces[k, t, :, :] * ok
                value = pieces[k, 2 + t, :, :]
                ec[1 + tile, 8:40, :] = value + 6.0
                tmp[...] = value[8:24, :]
                gathered[pl.ds(pl.multiple_of(128 + 8 * tile, 8), 8), :] = fold_rows(tmp, 8)

    def around_of(now, p, start, rows):
        here = slice(start, start + rows)
        upper_half = lane_iota(rows) >= 64
        value = now[p, here, :]
        ahead = pltpu.roll(jnp.where(upper_half, value, now[p + 1, here, :]), 64, 1)
        behind = pltpu.roll(jnp.where(upper_half, now[p - 1, here, :], value), 64, 1)
        total = (
            (pltpu.roll(value, LANES - 1, 1) + pltpu.roll(value, 1, 1))
            + (ahead + behind)
            + (now[p, start - 1 : start - 1 + rows, :] + now[p, start + 1 : start + 1 + rows, :])
        )
        return total, value

    now = es
    for k, table in enumerate(step_tables(smooth_top + 16.0 * absorb_top)):
        target = (a, b)[k % 2]
        ok_scaled = ok * table[0]

        for p in range(1, 17):
            for start in (8, 24):
                here = slice(start, start + 16)
                total, value = around_of(now, p, start, 16)
                target[p, here, :] = combine(
                    table, total, value, ec[p, here, :],
                    lambda: es[p, here, :],
                    lambda: target[p, here, :],
                    ok_scaled[start - 8 : start + 8, :],
                )
        now = target
    for t in range(2):
        it2[t, :, :] = now[1 + 2 * gx + t, 16:32, :]
    for t in range(16):
        around, value = around_of(now, 1 + t, 16, 16)
        tmp[...] = es[1 + t, 16:32, :] - ec[1 + t, 16:32, :] * value + around
        gathered[8 * t : 8 * t + 8, :] = fold_rows(tmp, 8)
    j = lax.broadcasted_iota(jnp.int32, (LANES, LANES), 0) % 64
    column = lax.broadcasted_iota(jnp.int32, (LANES, LANES), 1)
    goes_to = jnp.where((j >= 5) & (j < 37), (j - 5) // 2, -1)
    folded = exact_dot(gathered[...], jnp.where(goes_to == column, 0.5, 0.0).astype(F32))
    lane8 = lane_iota(8)
    for half in range(2):
        total = jnp.zeros((8, LANES), F32)
        for x in range(8):
            at = 8 * (8 * half + x)
            value = jnp.where(core == 0, folded[at : at + 8, :], folded[128 + at : 136 + at, :])
            total = jnp.where(lane8 // 16 == x, rolled(value, 16 * x), total)
        piece[half, :, :] = total


Z_SLOTS = (0, -1, 1, -3, -4, -2, 3, 2)


def bottom_kernel(mine, other, it2, out, s, c, a, b, window):
    gx, gy, gz = lax.axis_index("gx"), lax.axis_index("gy"), lax.axis_index("gz")
    core = gx % 2
    lane8 = lane_iota(8)
    lane = lane_iota(64)
    for ref in (s, a, b):
        clear_pads(ref, 10, 8, 72)

    def unpack(slot, carry):
        offset = jnp.int32(0)
        for n, o in enumerate(Z_SLOTS):
            offset = jnp.where(slot == n, o, offset)
        z_owner = (gz + offset + 8) % 8
        at = pl.multiple_of(8 + 8 * z_owner, 8)
        for kind, ref in enumerate((s, c)):
            for x in range(8):
                total = jnp.zeros((8, LANES), F32)
                for m in range(4):
                    y_owner = (gy - m + 4) % 4
                    for half in range(2):
                        value = jnp.where(
                            core == kind, mine[m, slot, half, :, :], other[m, slot, half, :, :]
                        )
                        start = 64 * half + 16 * y_owner
                        value = pltpu.roll(value, (start - 16 * x + LANES) % LANES, 1)
                        total = jnp.where(lane8 // 16 == 4 * half + y_owner, value, total)
                ref[1 + x, pl.ds(at, 8), :] = total if kind == 0 else total + 6.0
        return carry

    lax.fori_loop(0, 8, unpack, 0)

    def wrap(ref):
        ref[0, 8:72, :] = jnp.where(lane >= 64, pltpu.roll(ref[8, 8:72, :], 64, 1), 0.0)
        ref[9, 8:72, :] = jnp.where(lane < 64, pltpu.roll(ref[1, 8:72, :], 64, 1), 0.0)

    top = smooth_top + 4.0**LEVELS * absorb_top
    lane16 = lane_iota(16)
    keep_right = jnp.where(lane16 % 64 == 63, 0.0, 1.0)
    keep_left = jnp.where(lane16 % 64 == 0, 0.0, 1.0)
    now = s
    for k, table in enumerate(step_tables(top, BOTTOM_ITERS, bottom_low)):
        target = (a, b)[k % 2]
        for p in (4, 5, 3, 6, 2, 7, 1, 8):
            if p == 1:
                wrap(now)
            for start in range(8, 72, 16):
                here = slice(start, start + 16)
                value = now[p, here, :]
                around = (
                    pltpu.roll(value, LANES - 1, 1) * keep_right
                    + pltpu.roll(value, 1, 1) * keep_left
                    + (now[p - 1, here, :] + now[p + 1, here, :])
                    + (now[p, start - 1 : start + 15, :] + now[p, start + 1 : start + 17, :])
                )
                scale, pull, lift, back = table
                inner = around - c[p, here, :] * value
                if lift:
                    inner = inner + (s[p, here, :] if lift == 1.0 else lift * s[p, here, :])
                new = (scale * pull) * value + scale * inner
                if back:
                    new = new - back * target[p, here, :]
                target[p, here, :] = new
        now = target
    row24 = row_iota(24)
    lane24 = lane_iota(24)
    low_row = pl.multiple_of(8 * gz, 8)
    rows_ok = ((row24 >= 8) | (gz > 0)) & ((row24 < 16) | (gz < 7))
    lanes_ok = ((lane24 >= 1) | (gy > 0)) & ((lane24 <= 16) | (gy < 3)) & (lane24 < 18)
    row = lax.broadcasted_iota(jnp.int32, (LANES, LANES), 0)
    column = lax.broadcasted_iota(jnp.int32, (LANES, LANES), 1)
    center = column // 2 + 1
    side = jnp.where(column % 2 == 0, center - 1, center + 1)
    spread = jnp.where(row == center, 0.75, jnp.where(row == side, 0.25, 0.0))
    spread = jnp.where(column < 32, spread, 0.0).astype(F32)
    for j in range(4):
        x = 2 * gx - 1 + j
        x_ok = (x >= 0) & (x < 16)
        xc = jnp.clip(x, 0, 15)
        value = now[1 + xc % 8, pl.ds(low_row, 24), :]
        amount = (2 * LANES - 64 * (xc // 8) - 16 * gy + 1) % LANES
        value = pltpu.roll(value, amount, 1)
        value = jnp.where(rows_ok & lanes_ok & x_ok, value, 0.0)
        window[24 * j : 24 * j + 24, :] = value
    wide = exact_dot(window[...], spread)
    planes = [wide[24 * j : 24 * j + 24, :] for j in range(4)]
    for i in range(4):
        base = i // 2 + 1
        near = base - 1 if i % 2 == 0 else base + 1
        mixed = 0.75 * planes[base] + 0.25 * planes[near]
        window[0:24, :] = mixed
        even = 0.75 * window[8:16, :] + 0.25 * window[7:15, :]
        odd = 0.75 * window[8:16, :] + 0.25 * window[9:17, :]
        window[pl.ds(32, 8, stride=2), :] = even
        window[pl.ds(33, 8, stride=2), :] = odd
        own = rolled(it2[i // 2, :, :], -5 - 64 * (i % 2))
        out[i, :, :] = (own + window[32:48, :])[:, 0:32]


def exchange(low, high, axis):
    return shift(high, axis, 1), shift(low, axis, -1)


def on_device(rs, ab):
    low, high, c1 = call(
        before_kernel,
        [(10, 64, LANES)] * 2 + [(4, 32, LANES)],
        [(64, LANES), (256, LANES)],
        rs, ab,
    )
    fl, fr = exchange(low, high, "gx")
    low, high = call(z_strips_kernel, [(358, LANES)] * 2, [], rs, ab, c1, fl, fr)
    zl, zh = exchange(low, high, "gz")
    es, ec, low, high, c1e = call(
        build0_kernel,
        [(26, 96, LANES)] * 2 + [(288, LANES)] * 2 + [(8, 64, LANES)],
        [],
        rs, ab, c1, fl, fr, zl, zh,
    )
    low0, high0 = exchange(low, high, "gy")
    it0, s1, low, high = call(
        level0_kernel,
        [(16, 64, LANES), (4, 32, LANES)] + [(3, 32, LANES)] * 2,
        [(26, 96, LANES)] * 2 + [(96, LANES)] * 6 + [(80, LANES)] * 3 + [(64, LANES), (256, LANES)],
        es, ec, low, high, low0, high0,
    )
    fl, fr = exchange(low, high, "gx")
    low, high = call(z_strips1_kernel, [(144, LANES)] * 2, [], s1, fl, fr)
    zl, zh = exchange(low, high, "gz")
    ext, low, high = call(
        build1_kernel,
        [(9, 64, LANES)] + [(128, LANES)] * 2,
        [],
        s1, fl, fr, zl, zh,
    )
    yl, yh = exchange(low, high, "gy")
    it1, piece = call(
        level1_kernel,
        [(8, 32, 64), (4, 32, LANES)],
        [(18, 80, LANES)] * 4 + [(64, LANES), (256, LANES)],
        ext, yl, yh, c1e, low0, high0,
    )
    chips = jnp.stack([piece] + [shift(piece, "gx", 2 * k) for k in range(1, 4)])
    others = lax.ppermute(chips, "gx", [(i, i ^ 1) for i in range(8)])
    it2, piece = call(
        level2_kernel,
        [(2, 16, LANES), (2, 8, LANES)],
        [(18, 48, LANES)] * 4 + [(16, LANES), (256, LANES)],
        chips, others,
    )
    near = jnp.stack((piece, shift(piece, "gz", 1), shift(piece, "gz", -1)))
    column = jnp.concatenate((near, shift(near, "gz", 3), shift(near[:2], "gz", -3)))
    grid = jnp.stack([column] + [shift(column, "gy", k) for k in range(1, 4)])
    other = lax.ppermute(grid, "gx", [(i, i ^ 1) for i in range(8)])
    (corrected,) = call(
        bottom_kernel,
        [(4, 16, 32)],
        [(10, 80, LANES)] * 4 + [(96, LANES)],
        grid, other, it2,
    )
    return it0, it1, corrected


def solution(mesh):
    placed = (P("gx", "gz", "gy"), P("gx", "gz", "gy"))
    return jax.shard_map(
        on_device,
        mesh=mesh,
        in_specs=placed,
        out_specs=(P("gx", "gz", "gy"), P("gx", "gz", "gy"), P("gx", "gz", "gy")),
        check_vma=False,
    )
```

time: 980 us -> 105 us (0.11)
  the two profiles are of different devices: /device:TPU:2 before, /device:TPU:1 now
where the time goes in v2:
time: 105 us
  waiting for transfers between devices  44.2 us (42%)
  starting transfers between devices  38.8 us (37%)
  Pallas kernels  19.3 us (18%)
  local copies, waits for them, and re-layouts  2.09 us (2%)
    ppermute x22, waiting for transfers between devices, shift(): lax.ppermute(value, axis, [(i, (i + step) % count) for i in range(count)])  41.9 us
    ppermute x22, starting transfers between devices, shift(): lax.ppermute(value, axis, [(i, (i + step) % count) for i in range(count)])  33 us
    pallas_call x9, Pallas kernels, call(): pl.pallas_call(kernel, out_shape=[jax.ShapeDtypeStruct(s, F32) for s in o...  19.3 us
    ppermute x1, starting transfers between devices, on_device(): other = lax.ppermute(grid, 'gx', [(i, i ^ 1) for i in range(8)])  4.7 us
  transfers between devices with their start and end apart: 24, of which 19 were waited for; matrix products, arithmetic and copies ran while one was open for 0% of the time, Pallas kernels for 0%

profile of v2, /device:TPU:1, one launch (start us, length us, event | category | flops | bytes accessed | tf_op | source)
XLA Modules:
  0.0 105.1 jit_solution(5289360931422944009)
XLA Ops:
  0.6 1.0 copy-done
  1.7 1.0 copy-done.1
  2.7 0.3 shard_map.49
  3.1 2.6 %collective-permute-start = (f32[10,64,128]{2,1,0:T(8,128)S(1)}, f32[10,64,128]{2,1,0:T(8,128)S(1)}, u32[]{:S(2)}, u32[]{:S(2)}) collective-permute-start(f32[10,64,128]{2,1,0:T(8,128)S(1)} %get-tuple-element.27), channel_id=1, source_target_pairs={{0,32},{32,64},{64,96},{96,128},{128,160},{160,192},{192,224},{224... | collective-permute-start | bytes 983048 | tf_op jit(solution)/shard_map/ppermute | solution.py:40
  5.7 0.6 collective-permute-start.1
  6.3 3.4 %collective-permute-done.fl = f32[10,64,128]{2,1,0:T(8,128)S(1)} collective-permute-done((f32[10,64,128]{2,1,0:T(8,128)S(1)}, f32[10,64,128]{2,1,0:T(8,128)S(1)}, u32[]{:S(2)}, u32[]{:S(2)}) %collective-permute-start) | collective-permute-done | bytes 327712 | tf_op jit(solution)/shard_map/ppermute | solution.py:40
  9.7 2.8 %collective-permute-done.1.fr = f32[10,64,128]{2,1,0:T(8,128)S(1)} collective-permute-done((f32[10,64,128]{2,1,0:T(8,128)S(1)}, f32[10,64,128]{2,1,0:T(8,128)S(1)}, u32[]{:S(2)}, u32[]{:S(2)}) %collective-permute-start.1) | collective-permute-done | bytes 327712 | tf_op jit(solution)/shard_map/ppermute | solution.py:40
  12.5 1.4 %collective-permute-start.2 = (f32[358,128]{1,0:T(8,128)S(1)}, f32[358,128]{1,0:T(8,128)S(1)}, u32[]{:S(2)}, u32[]{:S(2)}) collective-permute-start(f32[358,128]{1,0:T(8,128)S(1)} %get-tuple-element.29), channel_id=1, source_target_pairs={{0,1},{1,2},{2,3},{3,4},{4,5},{5,6},{6,7},{7,0},{8,9},{9,10},{10,1... | collective-permute-start | bytes 549896 | tf_op jit(solution)/shard_map/ppermute | solution.py:40
  13.9 4.0 %collective-permute-start.3 = (f32[358,128]{1,0:T(8,128)S(1)}, f32[358,128]{1,0:T(8,128)S(1)}, u32[]{:S(2)}, u32[]{:S(2)}) collective-permute-start(f32[358,128]{1,0:T(8,128)S(1)} %get-tuple-element.30), channel_id=1, source_target_pairs={{0,7},{1,0},{2,1},{3,2},{4,3},{5,4},{6,5},{7,6},{8,15},{9,8},{10,9... | collective-permute-start | bytes 549896 | tf_op jit(solution)/shard_map/ppermute | solution.py:40
  17.9 4.8 %collective-permute-done.2.zl = f32[358,128]{1,0:T(8,128)S(1)} collective-permute-done((f32[358,128]{1,0:T(8,128)S(1)}, f32[358,128]{1,0:T(8,128)S(1)}, u32[]{:S(2)}, u32[]{:S(2)}) %collective-permute-start.2) | collective-permute-done | bytes 183328 | tf_op jit(solution)/shard_map/ppermute | solution.py:40
  22.8 0.8 shard_map.51
  23.6 2.8 %collective-permute-start.5 = (f32[288,128]{1,0:T(8,128)S(1)}, f32[288,128]{1,0:T(8,128)S(1)}, u32[]{:S(2)}, u32[]{:S(2)}) collective-permute-start(f32[288,128]{1,0:T(8,128)S(1)} %get-tuple-element.33.low_sent), channel_id=1, source_target_pairs={{0,24},{8,0},{16,8},{24,16},{1,25},{9,1},{17,9},{25,17},{2,26},{10... | collective-permute-start | bytes 442376 | tf_op jit(solution)/shard_map/ppermute | solution.py:40
  26.4 2.5 %collective-permute-done.5.yh.high0 = f32[288,128]{1,0:T(8,128)S(1)} collective-permute-done((f32[288,128]{1,0:T(8,128)S(1)}, f32[288,128]{1,0:T(8,128)S(1)}, u32[]{:S(2)}, u32[]{:S(2)}) %collective-permute-start.5) | collective-permute-done | bytes 147488 | tf_op jit(solution)/shard_map/ppermute | solution.py:40
  28.9 3.1 %collective-permute-done.4.yl.low0 = f32[288,128]{1,0:T(8,128)S(1)} collective-permute-done((f32[288,128]{1,0:T(8,128)S(1)}, f32[288,128]{1,0:T(8,128)S(1)}, u32[]{:S(2)}, u32[]{:S(2)}) %collective-permute-start.4) | collective-permute-done | bytes 147488 | tf_op jit(solution)/shard_map/ppermute | solution.py:40
  32.0 6.6 %shard_map.52 = (f32[16,64,128]{2,1,0:T(8,128)}, f32[4,32,128]{2,1,0:T(8,128)S(1)}, f32[3,32,128]{2,1,0:T(8,128)S(1)}, f32[3,32,128]{2,1,0:T(8,128)S(1)}) custom-call(f32[26,96,128]{2,1,0:T(8,128)S(1)} %get-tuple-element.31.es, f32[26,96,128]{2,1,0:T(8,128)S(1)} %get-tuple-element.32.ec, f32[288,128]{1,0:T(8,128)S(1)} %get-tuple-element.33.low_sent, ...), custom_call_target="tpu_custom_call" | custom-call | tf_op jit(solution)/shard_map/pallas_call | solution.py:72
  38.7 2.0 %collective-permute-start.6 = (f32[3,32,128]{2,1,0:T(8,128)S(1)}, f32[3,32,128]{2,1,0:T(8,128)S(1)}, u32[]{:S(2)}, u32[]{:S(2)}) collective-permute-start(f32[3,32,128]{2,1,0:T(8,128)S(1)} %get-tuple-element.37), channel_id=1, source_target_pairs={{0,32},{32,64},{64,96},{96,128},{128,160},{160,192},{192,224},{224... | collective-permute-start | bytes 147464 | tf_op jit(solution)/shard_map/ppermute | solution.py:40
  40.7 1.2 %collective-permute-done.6.fl = f32[3,32,128]{2,1,0:T(8,128)S(1)} collective-permute-done((f32[3,32,128]{2,1,0:T(8,128)S(1)}, f32[3,32,128]{2,1,0:T(8,128)S(1)}, u32[]{:S(2)}, u32[]{:S(2)}) %collective-permute-start.6) | collective-permute-done | bytes 49184 | tf_op jit(solution)/shard_map/ppermute | solution.py:40
  41.9 2.6 %collective-permute-done.7.fr = f32[3,32,128]{2,1,0:T(8,128)S(1)} collective-permute-done((f32[3,32,128]{2,1,0:T(8,128)S(1)}, f32[3,32,128]{2,1,0:T(8,128)S(1)}, u32[]{:S(2)}, u32[]{:S(2)}) %collective-permute-start.7) | collective-permute-done | bytes 49184 | tf_op jit(solution)/shard_map/ppermute | solution.py:40
  44.5 0.1 shard_map.53
  44.6 3.0 %collective-permute-start.9 = (f32[144,128]{1,0:T(8,128)S(1)}, f32[144,128]{1,0:T(8,128)S(1)}, u32[]{:S(2)}, u32[]{:S(2)}) collective-permute-start(f32[144,128]{1,0:T(8,128)S(1)} %get-tuple-element.40), channel_id=1, source_target_pairs={{0,7},{1,0},{2,1},{3,2},{4,3},{5,4},{6,5},{7,6},{8,15},{9,8},{10,9... | collective-permute-start | bytes 221192 | tf_op jit(solution)/shard_map/ppermute | solution.py:40
  47.7 1.7 %collective-permute-done.8.zl = f32[144,128]{1,0:T(8,128)S(1)} collective-permute-done((f32[144,128]{1,0:T(8,128)S(1)}, f32[144,128]{1,0:T(8,128)S(1)}, u32[]{:S(2)}, u32[]{:S(2)}) %collective-permute-start.8) | collective-permute-done | bytes 73760 | tf_op jit(solution)/shard_map/ppermute | solution.py:40
  49.3 0.3 shard_map.54
  49.6 0.1 collective-permute-start.10
  49.7 2.7 %collective-permute-start.11 = (f32[128,128]{1,0:T(8,128)S(1)}, f32[128,128]{1,0:T(8,128)S(1)}, u32[]{:S(2)}, u32[]{:S(2)}) collective-permute-start(f32[128,128]{1,0:T(8,128)S(1)} %get-tuple-element.43), channel_id=1, source_target_pairs={{0,24},{8,0},{16,8},{24,16},{1,25},{9,1},{17,9},{25,17},{2,26},{10... | collective-permute-start | bytes 196616 | tf_op jit(solution)/shard_map/ppermute | solution.py:40
  52.4 1.6 %collective-permute-done.10.yl = f32[128,128]{1,0:T(8,128)S(1)} collective-permute-done((f32[128,128]{1,0:T(8,128)S(1)}, f32[128,128]{1,0:T(8,128)S(1)}, u32[]{:S(2)}, u32[]{:S(2)}) %collective-permute-start.10) | collective-permute-done | bytes 65568 | tf_op jit(solution)/shard_map/ppermute | solution.py:40
  54.0 3.1 %shard_map.55 = (f32[8,32,64]{2,1,0:T(8,128)}, f32[4,32,128]{2,1,0:T(8,128)S(1)}) custom-call(f32[9,64,128]{2,1,0:T(8,128)S(1)} %get-tuple-element.41.ext, f32[128,128]{1,0:T(8,128)S(1)} %collective-permute-done.10.yl, f32[128,128]{1,0:T(8,128)S(1)} %collective-permute-done.11.yh, f32[8,64,128]{2,1,0:T(8,128)S(1)} %get-tuple-element.44.c1e, ...), custom_call_target="tpu_custom_call" | custom-call | tf_op jit(solution)/shard_map/pallas_call | solution.py:72
  57.1 3.3 %collective-permute-start.14 = (f32[4,32,128]{2,1,0:T(8,128)S(1)}, f32[4,32,128]{2,1,0:T(8,128)S(1)}, u32[]{:S(2)}, u32[]{:S(2)}) collective-permute-start(f32[4,32,128]{2,1,0:T(8,128)S(1)} %get-tuple-element.46), channel_id=1, source_target_pairs={{0,192},{32,224},{64,0},{96,32},{128,64},{160,96},{192,128},{224,1... | collective-permute-start | bytes 196616 | tf_op jit(solution)/shard_map/ppermute | solution.py:40
  60.4 0.3 collective-permute-start.13
  60.8 0.3 collective-permute-start.12
  61.1 0.7 collective-permute-done.14
  61.8 3.4 %collective-permute-done.13 = f32[4,32,128]{2,1,0:T(8,128)S(1)} collective-permute-done((f32[4,32,128]{2,1,0:T(8,128)S(1)}, f32[4,32,128]{2,1,0:T(8,128)S(1)}, u32[]{:S(2)}, u32[]{:S(2)}) %collective-permute-start.13) | collective-permute-done | bytes 65568 | tf_op jit(solution)/shard_map/ppermute | solution.py:40
  65.1 1.7 %collective-permute-done.12 = f32[4,32,128]{2,1,0:T(8,128)S(1)} collective-permute-done((f32[4,32,128]{2,1,0:T(8,128)S(1)}, f32[4,32,128]{2,1,0:T(8,128)S(1)}, u32[]{:S(2)}, u32[]{:S(2)}) %collective-permute-start.12) | collective-permute-done | bytes 65568 | tf_op jit(solution)/shard_map/ppermute | solution.py:40
  66.9 1.1 %collective-permute-start.15 = (f32[4,4,32,128]{3,2,1,0:T(8,128)S(1)}, f32[4,4,32,128]{3,2,1,0:T(8,128)S(1)}, u32[]{:S(2)}, u32[]{:S(2)}) collective-permute-start(f32[4,4,32,128]{3,2,1,0:T(8,128)S(1)} %pad_maximum_fusion.mine), channel_id=1, source_target_pairs={{0,32},{32,0},{64,96},{96,64},{128,160},{160,128},{192,224},{224,1... | collective-permute-start | bytes 786440 | tf_op jit(solution)/shard_map/ppermute | solution.py:785
  68.0 1.2 %collective-permute-done.15.other = f32[4,4,32,128]{3,2,1,0:T(8,128)S(1)} collective-permute-done((f32[4,4,32,128]{3,2,1,0:T(8,128)S(1)}, f32[4,4,32,128]{3,2,1,0:T(8,128)S(1)}, u32[]{:S(2)}, u32[]{:S(2)}) %collective-permute-start.15) | collective-permute-done | bytes 262176 | tf_op jit(solution)/shard_map/ppermute | solution.py:785
  69.1 1.7 %shard_map.56 = (f32[2,16,128]{2,1,0:T(8,128)S(1)}, f32[2,8,128]{2,1,0:T(8,128)S(1)}) custom-call(f32[4,4,32,128]{3,2,1,0:T(8,128)S(1)} %pad_maximum_fusion.mine, f32[4,4,32,128]{3,2,1,0:T(8,128)S(1)} %collective-permute-done.15.other), custom_call_target="tpu_custom_call" | custom-call | tf_op jit(solution)/shard_map/pallas_call | solution.py:72
  70.8 3.1 %collective-permute-start.17 = (f32[2,8,128]{2,1,0:T(8,128)S(1)}, f32[2,8,128]{2,1,0:T(8,128)S(1)}, u32[]{:S(2)}, u32[]{:S(2)}) collective-permute-start(f32[2,8,128]{2,1,0:T(8,128)S(1)} %get-tuple-element.47), channel_id=1, source_target_pairs={{0,7},{1,0},{2,1},{3,2},{4,3},{5,4},{6,5},{7,6},{8,15},{9,8},{10,9... | collective-permute-start | bytes 24584 | tf_op jit(solution)/shard_map/ppermute | solution.py:40
  73.9 3.7 %collective-permute-done.16 = f32[2,8,128]{2,1,0:T(8,128)S(1)} collective-permute-done((f32[2,8,128]{2,1,0:T(8,128)S(1)}, f32[2,8,128]{2,1,0:T(8,128)S(1)}, u32[]{:S(2)}, u32[]{:S(2)}) %collective-permute-start.16) | collective-permute-done | bytes 8224 | tf_op jit(solution)/shard_map/ppermute | solution.py:40
  77.7 1.9 %collective-permute-start.19 = (f32[2,2,8,128]{3,2,1,0:T(8,128)S(1)}, f32[2,2,8,128]{3,2,1,0:T(8,128)S(1)}, u32[]{:S(2)}, u32[]{:S(2)}) collective-permute-start(f32[2,2,8,128]{3,2,1,0:T(8,128)S(1)} %pad_maximum_fusion.3), channel_id=1, source_target_pairs={{0,5},{1,6},{2,7},{3,0},{4,1},{5,2},{6,3},{7,4},{8,13},{9,14},{10,... | collective-permute-start | bytes 49160 | tf_op jit(solution)/shard_map/ppermute | solution.py:40
  79.6 1.4 %collective-permute-start.18 = (f32[3,2,8,128]{3,2,1,0:T(8,128)S(1)}, f32[3,2,8,128]{3,2,1,0:T(8,128)S(1)}, u32[]{:S(2)}, u32[]{:S(2)}) collective-permute-start(f32[3,2,8,128]{3,2,1,0:T(8,128)S(1)} %pad_maximum_fusion.2), channel_id=1, source_target_pairs={{0,3},{1,4},{2,5},{3,6},{4,7},{5,0},{6,1},{7,2},{8,11},{9,12},{10,... | collective-permute-start | bytes 73736 | tf_op jit(solution)/shard_map/ppermute | solution.py:40
  81.0 4.3 %collective-permute-done.18 = f32[3,2,8,128]{3,2,1,0:T(8,128)S(1)} collective-permute-done((f32[3,2,8,128]{3,2,1,0:T(8,128)S(1)}, f32[3,2,8,128]{3,2,1,0:T(8,128)S(1)}, u32[]{:S(2)}, u32[]{:S(2)}) %collective-permute-start.18) | collective-permute-done | bytes 24608 | tf_op jit(solution)/shard_map/ppermute | solution.py:40
  85.4 2.5 %collective-permute-start.22 = (f32[8,2,8,128]{3,2,1,0:T(8,128)S(1)}, f32[8,2,8,128]{3,2,1,0:T(8,128)S(1)}, u32[]{:S(2)}, u32[]{:S(2)}) collective-permute-start(f32[8,2,8,128]{3,2,1,0:T(8,128)S(1)} %constant_dynamic-update-slice_fusion), channel_id=1, source_target_pairs={{0,24},{8,0},{16,8},{24,16},{1,25},{9,1},{17,9},{25,17},{2,26},{10... | collective-permute-start | bytes 196616 | tf_op jit(solution)/shard_map/ppermute | solution.py:40
  87.9 0.7 collective-permute-start.20
  88.6 0.7 collective-permute-done.22
  89.2 3.4 %collective-permute-done.21 = f32[8,2,8,128]{3,2,1,0:T(8,128)S(1)} collective-permute-done((f32[8,2,8,128]{3,2,1,0:T(8,128)S(1)}, f32[8,2,8,128]{3,2,1,0:T(8,128)S(1)}, u32[]{:S(2)}, u32[]{:S(2)}) %collective-permute-start.21) | collective-permute-done | bytes 65568 | tf_op jit(solution)/shard_map/ppermute | solution.py:40
  92.6 0.3 collective-permute-done.20
  93.0 4.7 %collective-permute-start.23 = (f32[4,8,2,8,128]{4,3,2,1,0:T(8,128)S(1)}, f32[4,8,2,8,128]{4,3,2,1,0:T(8,128)S(1)}, u32[]{:S(2)}, u32[]{:S(2)}) collective-permute-start(f32[4,8,2,8,128]{4,3,2,1,0:T(8,128)S(1)} %pad_maximum_fusion.1.mine), channel_id=1, source_target_pairs={{0,32},{32,0},{64,96},{96,64},{128,160},{160,128},{192,224},{224,1... | collective-permute-start | bytes 786440 | tf_op jit(solution)/shard_map/ppermute | solution.py:795
  97.7 1.2 %collective-permute-done.23.other = f32[4,8,2,8,128]{4,3,2,1,0:T(8,128)S(1)} collective-permute-done((f32[4,8,2,8,128]{4,3,2,1,0:T(8,128)S(1)}, f32[4,8,2,8,128]{4,3,2,1,0:T(8,128)S(1)}, u32[]{:S(2)}, u32[]{:S(2)}) %collective-permute-start.23) | collective-permute-done | bytes 262176 | tf_op jit(solution)/shard_map/ppermute | solution.py:795
  98.8 6.3 %shard_map.57 = f32[4,16,32]{2,1,0:T(8,128)} custom-call(f32[4,8,2,8,128]{4,3,2,1,0:T(8,128)S(1)} %pad_maximum_fusion.1.mine, f32[4,8,2,8,128]{4,3,2,1,0:T(8,128)S(1)} %collective-permute-done.23.other, f32[2,16,128]{2,1,0:T(8,128)S(1)} %get-tuple-element.48.it2), custom_call_target="tpu_custom_call" | custom-call | tf_op jit(solution)/shard_map/pallas_call | solution.py:72
  (22 shorter events, 0.2 us)
Async XLA Ops:
  0.6 1.0 copy-start
  1.7 1.0 copy-start.1
  3.1 6.6 %collective-permute-start = (f32[10,64,128]{2,1,0:T(8,128)S(1)}, f32[10,64,128]{2,1,0:T(8,128)S(1)}, u32[]{:S(2)}, u32[]{:S(2)}) collective-permute-start(f32[10,64,128]{2,1,0:T(8,128)S(1)} %get-tuple-element.27), channel_id=1, source_target_pairs={{0,32},{32,64},{64,96},{96,128},{128,160},{160,192},{192,224},{224... | collective-permute-start | bytes 983048 | tf_op jit(solution)/shard_map/ppermute | solution.py:40
  5.7 6.8 %collective-permute-start.1 = (f32[10,64,128]{2,1,0:T(8,128)S(1)}, f32[10,64,128]{2,1,0:T(8,128)S(1)}, u32[]{:S(2)}, u32[]{:S(2)}) collective-permute-start(f32[10,64,128]{2,1,0:T(8,128)S(1)} %get-tuple-element.28), channel_id=1, source_target_pairs={{0,224},{32,0},{64,32},{96,64},{128,96},{160,128},{192,160},{224,1... | collective-permute-start | bytes 983048 | tf_op jit(solution)/shard_map/ppermute | solution.py:40
  12.5 10.3 %collective-permute-start.2 = (f32[358,128]{1,0:T(8,128)S(1)}, f32[358,128]{1,0:T(8,128)S(1)}, u32[]{:S(2)}, u32[]{:S(2)}) collective-permute-start(f32[358,128]{1,0:T(8,128)S(1)} %get-tuple-element.29), channel_id=1, source_target_pairs={{0,1},{1,2},{2,3},{3,4},{4,5},{5,6},{6,7},{7,0},{8,9},{9,10},{10,1... | collective-permute-start | bytes 549896 | tf_op jit(solution)/shard_map/ppermute | solution.py:40
  13.9 8.8 %collective-permute-start.3 = (f32[358,128]{1,0:T(8,128)S(1)}, f32[358,128]{1,0:T(8,128)S(1)}, u32[]{:S(2)}, u32[]{:S(2)}) collective-permute-start(f32[358,128]{1,0:T(8,128)S(1)} %get-tuple-element.30), channel_id=1, source_target_pairs={{0,7},{1,0},{2,1},{3,2},{4,3},{5,4},{6,5},{7,6},{8,15},{9,8},{10,9... | collective-permute-start | bytes 549896 | tf_op jit(solution)/shard_map/ppermute | solution.py:40
  23.6 5.3 %collective-permute-start.5 = (f32[288,128]{1,0:T(8,128)S(1)}, f32[288,128]{1,0:T(8,128)S(1)}, u32[]{:S(2)}, u32[]{:S(2)}) collective-permute-start(f32[288,128]{1,0:T(8,128)S(1)} %get-tuple-element.33.low_sent), channel_id=1, source_target_pairs={{0,24},{8,0},{16,8},{24,16},{1,25},{9,1},{17,9},{25,17},{2,26},{10... | collective-permute-start | bytes 442376 | tf_op jit(solution)/shard_map/ppermute | solution.py:40
  26.4 5.6 %collective-permute-start.4 = (f32[288,128]{1,0:T(8,128)S(1)}, f32[288,128]{1,0:T(8,128)S(1)}, u32[]{:S(2)}, u32[]{:S(2)}) collective-permute-start(f32[288,128]{1,0:T(8,128)S(1)} %get-tuple-element.34.high_sent), channel_id=1, source_target_pairs={{0,8},{8,16},{16,24},{24,0},{1,9},{9,17},{17,25},{25,1},{2,10},{10... | collective-permute-start | bytes 442376 | tf_op jit(solution)/shard_map/ppermute | solution.py:40
  38.7 3.2 %collective-permute-start.6 = (f32[3,32,128]{2,1,0:T(8,128)S(1)}, f32[3,32,128]{2,1,0:T(8,128)S(1)}, u32[]{:S(2)}, u32[]{:S(2)}) collective-permute-start(f32[3,32,128]{2,1,0:T(8,128)S(1)} %get-tuple-element.37), channel_id=1, source_target_pairs={{0,32},{32,64},{64,96},{96,128},{128,160},{160,192},{192,224},{224... | collective-permute-start | bytes 147464 | tf_op jit(solution)/shard_map/ppermute | solution.py:40
  40.7 3.8 %collective-permute-start.7 = (f32[3,32,128]{2,1,0:T(8,128)S(1)}, f32[3,32,128]{2,1,0:T(8,128)S(1)}, u32[]{:S(2)}, u32[]{:S(2)}) collective-permute-start(f32[3,32,128]{2,1,0:T(8,128)S(1)} %get-tuple-element.38), channel_id=1, source_target_pairs={{0,224},{32,0},{64,32},{96,64},{128,96},{160,128},{192,160},{224,1... | collective-permute-start | bytes 147464 | tf_op jit(solution)/shard_map/ppermute | solution.py:40
  44.6 4.7 %collective-permute-start.8 = (f32[144,128]{1,0:T(8,128)S(1)}, f32[144,128]{1,0:T(8,128)S(1)}, u32[]{:S(2)}, u32[]{:S(2)}) collective-permute-start(f32[144,128]{1,0:T(8,128)S(1)} %get-tuple-element.39), channel_id=1, source_target_pairs={{0,1},{1,2},{2,3},{3,4},{4,5},{5,6},{6,7},{7,0},{8,9},{9,10},{10,1... | collective-permute-start | bytes 221192 | tf_op jit(solution)/shard_map/ppermute | solution.py:40
  44.6 4.7 %collective-permute-start.9 = (f32[144,128]{1,0:T(8,128)S(1)}, f32[144,128]{1,0:T(8,128)S(1)}, u32[]{:S(2)}, u32[]{:S(2)}) collective-permute-start(f32[144,128]{1,0:T(8,128)S(1)} %get-tuple-element.40), channel_id=1, source_target_pairs={{0,7},{1,0},{2,1},{3,2},{4,3},{5,4},{6,5},{7,6},{8,15},{9,8},{10,9... | collective-permute-start | bytes 221192 | tf_op jit(solution)/shard_map/ppermute | solution.py:40
  49.6 4.4 %collective-permute-start.10 = (f32[128,128]{1,0:T(8,128)S(1)}, f32[128,128]{1,0:T(8,128)S(1)}, u32[]{:S(2)}, u32[]{:S(2)}) collective-permute-start(f32[128,128]{1,0:T(8,128)S(1)} %get-tuple-element.42), channel_id=1, source_target_pairs={{0,8},{8,16},{16,24},{24,0},{1,9},{9,17},{17,25},{25,1},{2,10},{10... | collective-permute-start | bytes 196616 | tf_op jit(solution)/shard_map/ppermute | solution.py:40
  49.7 4.3 %collective-permute-start.11 = (f32[128,128]{1,0:T(8,128)S(1)}, f32[128,128]{1,0:T(8,128)S(1)}, u32[]{:S(2)}, u32[]{:S(2)}) collective-permute-start(f32[128,128]{1,0:T(8,128)S(1)} %get-tuple-element.43), channel_id=1, source_target_pairs={{0,24},{8,0},{16,8},{24,16},{1,25},{9,1},{17,9},{25,17},{2,26},{10... | collective-permute-start | bytes 196616 | tf_op jit(solution)/shard_map/ppermute | solution.py:40
  57.1 4.6 %collective-permute-start.14 = (f32[4,32,128]{2,1,0:T(8,128)S(1)}, f32[4,32,128]{2,1,0:T(8,128)S(1)}, u32[]{:S(2)}, u32[]{:S(2)}) collective-permute-start(f32[4,32,128]{2,1,0:T(8,128)S(1)} %get-tuple-element.46), channel_id=1, source_target_pairs={{0,192},{32,224},{64,0},{96,32},{128,64},{160,96},{192,128},{224,1... | collective-permute-start | bytes 196616 | tf_op jit(solution)/shard_map/ppermute | solution.py:40
  60.4 4.7 %collective-permute-start.13 = (f32[4,32,128]{2,1,0:T(8,128)S(1)}, f32[4,32,128]{2,1,0:T(8,128)S(1)}, u32[]{:S(2)}, u32[]{:S(2)}) collective-permute-start(f32[4,32,128]{2,1,0:T(8,128)S(1)} %get-tuple-element.46), channel_id=1, source_target_pairs={{0,128},{32,160},{64,192},{96,224},{128,0},{160,32},{192,64},{224,... | collective-permute-start | bytes 196616 | tf_op jit(solution)/shard_map/ppermute | solution.py:40
  60.8 6.1 %collective-permute-start.12 = (f32[4,32,128]{2,1,0:T(8,128)S(1)}, f32[4,32,128]{2,1,0:T(8,128)S(1)}, u32[]{:S(2)}, u32[]{:S(2)}) collective-permute-start(f32[4,32,128]{2,1,0:T(8,128)S(1)} %get-tuple-element.46), channel_id=1, source_target_pairs={{0,64},{32,96},{64,128},{96,160},{128,192},{160,224},{192,0},{224,... | collective-permute-start | bytes 196616 | tf_op jit(solution)/shard_map/ppermute | solution.py:40
  66.9 2.3 %collective-permute-start.15 = (f32[4,4,32,128]{3,2,1,0:T(8,128)S(1)}, f32[4,4,32,128]{3,2,1,0:T(8,128)S(1)}, u32[]{:S(2)}, u32[]{:S(2)}) collective-permute-start(f32[4,4,32,128]{3,2,1,0:T(8,128)S(1)} %pad_maximum_fusion.mine), channel_id=1, source_target_pairs={{0,32},{32,0},{64,96},{96,64},{128,160},{160,128},{192,224},{224,1... | collective-permute-start | bytes 786440 | tf_op jit(solution)/shard_map/ppermute | solution.py:785
  70.8 6.8 %collective-permute-start.17 = (f32[2,8,128]{2,1,0:T(8,128)S(1)}, f32[2,8,128]{2,1,0:T(8,128)S(1)}, u32[]{:S(2)}, u32[]{:S(2)}) collective-permute-start(f32[2,8,128]{2,1,0:T(8,128)S(1)} %get-tuple-element.47), channel_id=1, source_target_pairs={{0,7},{1,0},{2,1},{3,2},{4,3},{5,4},{6,5},{7,6},{8,15},{9,8},{10,9... | collective-permute-start | bytes 24584 | tf_op jit(solution)/shard_map/ppermute | solution.py:40
  73.9 3.7 %collective-permute-start.16 = (f32[2,8,128]{2,1,0:T(8,128)S(1)}, f32[2,8,128]{2,1,0:T(8,128)S(1)}, u32[]{:S(2)}, u32[]{:S(2)}) collective-permute-start(f32[2,8,128]{2,1,0:T(8,128)S(1)} %get-tuple-element.47), channel_id=1, source_target_pairs={{0,1},{1,2},{2,3},{3,4},{4,5},{5,6},{6,7},{7,0},{8,9},{9,10},{10,1... | collective-permute-start | bytes 24584 | tf_op jit(solution)/shard_map/ppermute | solution.py:40
  77.7 7.7 %collective-permute-start.19 = (f32[2,2,8,128]{3,2,1,0:T(8,128)S(1)}, f32[2,2,8,128]{3,2,1,0:T(8,128)S(1)}, u32[]{:S(2)}, u32[]{:S(2)}) collective-permute-start(f32[2,2,8,128]{3,2,1,0:T(8,128)S(1)} %pad_maximum_fusion.3), channel_id=1, source_target_pairs={{0,5},{1,6},{2,7},{3,0},{4,1},{5,2},{6,3},{7,4},{8,13},{9,14},{10,... | collective-permute-start | bytes 49160 | tf_op jit(solution)/shard_map/ppermute | solution.py:40
  79.6 5.8 %collective-permute-start.18 = (f32[3,2,8,128]{3,2,1,0:T(8,128)S(1)}, f32[3,2,8,128]{3,2,1,0:T(8,128)S(1)}, u32[]{:S(2)}, u32[]{:S(2)}) collective-permute-start(f32[3,2,8,128]{3,2,1,0:T(8,128)S(1)} %pad_maximum_fusion.2), channel_id=1, source_target_pairs={{0,3},{1,4},{2,5},{3,6},{4,7},{5,0},{6,1},{7,2},{8,11},{9,12},{10,... | collective-permute-start | bytes 73736 | tf_op jit(solution)/shard_map/ppermute | solution.py:40
  85.4 3.9 %collective-permute-start.22 = (f32[8,2,8,128]{3,2,1,0:T(8,128)S(1)}, f32[8,2,8,128]{3,2,1,0:T(8,128)S(1)}, u32[]{:S(2)}, u32[]{:S(2)}) collective-permute-start(f32[8,2,8,128]{3,2,1,0:T(8,128)S(1)} %constant_dynamic-update-slice_fusion), channel_id=1, source_target_pairs={{0,24},{8,0},{16,8},{24,16},{1,25},{9,1},{17,9},{25,17},{2,26},{10... | collective-permute-start | bytes 196616 | tf_op jit(solution)/shard_map/ppermute | solution.py:40
  87.9 4.7 %collective-permute-start.21 = (f32[8,2,8,128]{3,2,1,0:T(8,128)S(1)}, f32[8,2,8,128]{3,2,1,0:T(8,128)S(1)}, u32[]{:S(2)}, u32[]{:S(2)}) collective-permute-start(f32[8,2,8,128]{3,2,1,0:T(8,128)S(1)} %constant_dynamic-update-slice_fusion), channel_id=1, source_target_pairs={{0,16},{8,24},{16,0},{24,8},{1,17},{9,25},{17,1},{25,9},{2,18},{10... | collective-permute-start | bytes 196616 | tf_op jit(solution)/shard_map/ppermute | solution.py:40
  87.9 5.0 %collective-permute-start.20 = (f32[8,2,8,128]{3,2,1,0:T(8,128)S(1)}, f32[8,2,8,128]{3,2,1,0:T(8,128)S(1)}, u32[]{:S(2)}, u32[]{:S(2)}) collective-permute-start(f32[8,2,8,128]{3,2,1,0:T(8,128)S(1)} %constant_dynamic-update-slice_fusion), channel_id=1, source_target_pairs={{0,8},{8,16},{16,24},{24,0},{1,9},{9,17},{17,25},{25,1},{2,10},{10... | collective-permute-start | bytes 196616 | tf_op jit(solution)/shard_map/ppermute | solution.py:40
  93.0 5.9 %collective-permute-start.23 = (f32[4,8,2,8,128]{4,3,2,1,0:T(8,128)S(1)}, f32[4,8,2,8,128]{4,3,2,1,0:T(8,128)S(1)}, u32[]{:S(2)}, u32[]{:S(2)}) collective-permute-start(f32[4,8,2,8,128]{4,3,2,1,0:T(8,128)S(1)} %pad_maximum_fusion.1.mine), channel_id=1, source_target_pairs={{0,32},{32,0},{64,96},{96,64},{128,160},{160,128},{192,224},{224,1... | collective-permute-start | bytes 786440 | tf_op jit(solution)/shard_map/ppermute | solution.py:795
